TPU v7x, 32 devices: a whole 2x2x4 slice. The times are simulated.
32 devices in a mesh: lag: 8 (over y, x, core), row: 4 (over z).
Axes of the slice: x: 2, y: 2, z: 4, core: 2. Of those that a mesh axis runs over, the one named last changes fastest.
Arguments:
- lag_matrix: bfloat16 [8, 8192, 8192], P('lag', 'row'), may hold values from -0.0234375 to 0.0234375
- past_current: bfloat16 [8, 256, 8192], P('lag', None, 'row'), may hold values from -6 to 6
- excitation: float32 [2, 256, 8192], P(None, None, 'row'), may hold values from -6 to 6
- block_inverse: float32 [64, 128, 128], P('row'), may hold values from -2 to 3
Outputs:
- currents: bfloat16 [2, 256, 8192], P(None, 'lag', 'row')
All inputs are finite; a program needn't handle non-finite values.
Results may differ from a plain program's by a relative error of at most 0.002.
Values may be sent and summed in bfloat16 or wider, within the bound.
No kernel may reach another device: no remote copies, remote signals or barrier semaphores. Data moves between devices by JAX's collectives and lax.ppermute only.
A program may use at most 128 MiB of HBM per device.

v0:
```python
import functools

import jax
import jax.numpy as jnp
from jax import lax
from jax.experimental import pallas as pl
from jax.experimental.pallas import tpu as pltpu
from jax.sharding import PartitionSpec as P

PIECES = 2


def product_kernel(idx, *refs, count, groups, add):
    xs, a_ref = refs[:count], refs[count]
    rest = list(refs[count + 1 :])
    c_refs = [rest.pop(0) for _ in range(groups)] if add else None
    o_refs = [rest.pop(0) for _ in range(groups)]
    buf = xs[0]
    if count > 1:
        buf = rest.pop(0)

        @pl.when(pl.program_id(0) == 0)
        def _():
            at = 0
            for x in xs:
                buf[at : at + x.shape[0]] = x[...]
                at += x.shape[0]

    def put(values):
        at = 0
        for k, o in enumerate(o_refs):
            rows = o.shape[1]
            if values is None:
                o[0] = c_refs[k][0]
            elif add:
                o[0] = c_refs[k][0] + values[at : at + rows]
            else:
                o[0] = values[at : at + rows]
            at += rows

    def value():
        return lax.dot_general(
            buf[...], a_ref[...], (((1,), (1,)), ((), ())), preferred_element_type=jnp.float32
        )

    if not add:
        put(value())
        return

    @pl.when(idx[2] != 0)
    def _():
        put(value())

    @pl.when(idx[2] == 0)
    def _():
        put(None)


def product(idx, xs, matrix, totals=None, side=None, groups=1):
    count, width = len(xs), xs[0].shape[1]
    rows = sum(x.shape[0] for x in xs)
    each = rows // groups
    half = matrix.shape[0] // 2
    first, steps = (0, 2) if side is None else (side, 1)
    in_specs = [pl.BlockSpec(x.shape, lambda t, s: (0, 0)) for x in xs]
    in_specs.append(pl.BlockSpec((half, width), lambda t, s: ((1 - s[1] + t + first) % 2, s[0])))
    operands = [*xs, matrix]
    if totals is not None:
        in_specs += [pl.BlockSpec((1, each, half), lambda t, s: (t + first, 0, 0))] * groups
        operands += totals
    scratch = [pltpu.VMEM((rows, width), xs[0].dtype)] if count > 1 else []
    return pl.pallas_call(
        functools.partial(product_kernel, count=count, groups=groups, add=totals is not None),
        out_shape=[jax.ShapeDtypeStruct((steps, each, half), jnp.float32)] * groups,
        grid_spec=pltpu.PrefetchScalarGridSpec(
            num_scalar_prefetch=1,
            grid=(steps,),
            in_specs=in_specs,
            out_specs=[pl.BlockSpec((1, each, half), lambda t, s: (t, 0, 0))] * groups,
            scratch_shapes=scratch,
        ),
        compiler_params=pltpu.CompilerParams(
            dimension_semantics=("arbitrary",), vmem_limit_bytes=36 << 20
        ),
        cost_estimate=pl.CostEstimate(
            flops=2 * rows * steps * half * width,
            bytes_accessed=steps * half * (2 * width + 8 * rows),
            transcendentals=0,
        ),
    )(idx, *operands)


def solve_blocks(source, inverse):
    count = source.shape[0]
    pieces = source.reshape(count, inverse.shape[0], inverse.shape[1])
    result = jnp.einsum("bij,rbj->rbi", inverse, pieces, precision=lax.Precision.HIGHEST)
    return result.reshape(count, source.shape[1]).astype(jnp.bfloat16)


def line_slots(x, row, rows):
    cut = x.shape[0] // PIECES
    left = right = [x[k * cut : (k + 1) * cut] for k in range(PIECES)]
    yield [x], row, row >= 0, list(range(rows))

    def send(pieces, pairs):
        out = []
        for piece in pieces:
            out.append(lax.ppermute(piece, "row", pairs))
        return out

    for step in range(1, rows):
        up = list(range(step - 1, rows - 1))
        down = list(range(1, rows - step + 1))
        from_left = [i + 1 for i in up]
        from_right = [i - 1 for i in down]
        up_pairs = [(i, i + 1) for i in up]
        down_pairs = [(i, i - 1) for i in down]
        if set(up) & set(down):
            left = send(left, up_pairs)
            right = send(right, down_pairs)
            if set(from_left) & set(from_right):
                yield left, jnp.maximum(row - step, 0), row >= step, from_left
                yield right, jnp.minimum(row + step, rows - 1), row + step < rows, from_right
                continue
            left = right = [jnp.where(row >= step, a, b) for a, b in zip(left, right)]
        else:
            left = right = send(left, up_pairs + down_pairs)
        block = jnp.where(row >= step, row - step, jnp.minimum(row + step, rows - 1))
        yield left, block, (row >= step) | (row + step < rows), from_left + from_right


def per_device(lag_matrix, past_current, excitation, block_inverse):
    lags, rows = lax.axis_size("lag"), lax.axis_size("row")
    lag, row = lax.axis_index("lag"), lax.axis_index("row")
    chips, chip, core = lags // 2, lag // 2, lag % 2
    matrix = lag_matrix[0]
    own = past_current[0]
    excite, width = own.shape
    half = width // 2
    blocks = block_inverse.shape[0] // 2
    share = excite // chips
    inverse = lax.dynamic_slice_in_dim(block_inverse, core * blocks, blocks, 0)
    drive = lax.dynamic_slice(
        excitation, (0, chip * share, core * half), (excitation.shape[0], share, half)
    )
    mate = [(i, i ^ 1) for i in range(lags)]

    def index(block, flag):
        return jnp.stack([block, core, flag.astype(jnp.int32)])

    def older(value, senders):
        pairs = [
            (k * rows + i, (k + 1) * rows + i) for k in range(lags - 1) for i in senders
        ]
        return lax.ppermute(value, ("lag", "row"), pairs)

    def halves(xs, idx, total):
        (other,) = product(idx, xs, matrix, total, 0)
        got = lax.ppermute(other, "lag", mate)
        (mine,) = product(idx, xs, matrix, total, 1)
        return mine + got

    def reduce_chips(pair):
        pair = pair.reshape(chips, share, half)
        total = lax.dynamic_index_in_dim(pair, chip, 0, keepdims=False)
        for d in range(1, chips):
            sent = lax.dynamic_index_in_dim(pair, chip ^ d, 0, keepdims=False)
            total += lax.ppermute(sent, "lag", [(i, i ^ (2 * d)) for i in range(lags)])
        return total

    total = None
    slots = list(line_slots(own, row, rows))
    for pieces, block, valid, senders in slots[:-1]:
        value = pieces[0] if len(pieces) == 1 else jnp.concatenate(pieces, axis=0)
        total = product(
            index(block, valid), [value, older(value, senders)], matrix, total, groups=2
        )
    pieces, block, valid, senders = slots[-1]
    idx = index(block, valid)
    pair = halves(pieces, idx, total[:1])
    news = solve_blocks(drive[0] - reduce_chips(pair), inverse)
    late = [older(piece, senders) for piece in pieces]
    second = product(idx, late, matrix, total[1:])

    beside = lax.ppermute(news, "lag", mate)
    whole = jnp.concatenate(
        [jnp.where(core == 0, news, beside), jnp.where(core == 0, beside, news)], axis=1
    )
    far = [k for k in range(1, chips) if k & (k - 1)]
    near = [k for k in range(1, chips) if not k & (k - 1)]

    def to_first(x, k):
        return lax.ppermute(x, "lag", [(2 * k, 0)])

    def along(x, d, which):
        pairs = [(k * rows + i, k * rows + (i ^ d)) for k in which for i in range(rows)]
        return lax.ppermute(x, ("lag", "row"), pairs)

    near_here = [to_first(whole, k) for k in near]
    far_here = [to_first(whole, k) for k in far]
    away = [along(whole, d, [2 * k for k in [0] + near]) for d in range(1, rows)]
    far_stack = jnp.concatenate(far_here, axis=0)
    far_away = [far_stack] + [along(far_stack, d, [0]) for d in range(1, rows)]
    near_away = [[to_first(away[d - 1], k) for k in near] for d in range(1, rows)]
    first = lag == 0
    order = [0] + far + near
    for d in range(rows):
        if d == 0:
            one, close = whole, near_here
        else:
            one = away[d - 1]
            close = near_away[d - 1]
        fars = [far_away[d][j * share : (j + 1) * share] for j in range(len(far))]
        parts = [one] + fars + close
        parts = [parts[order.index(k)] for k in range(chips)]
        idx = index(row ^ d, first)
        if d < rows - 1:
            second = product(idx, parts, matrix, second)
        else:
            pair = halves(parts, idx, second)
    finals = solve_blocks(drive[1] - reduce_chips(pair), inverse)
    beside = lax.ppermute(finals, "lag", mate)
    final = jnp.concatenate(
        [jnp.where(core == 0, finals, beside), jnp.where(core == 0, beside, finals)], axis=1
    )
    count = share // 2
    return jnp.stack(
        [lax.dynamic_slice_in_dim(x, core * count, count, 0) for x in (whole, final)]
    )


def solution(mesh):
    in_specs = (
        P("lag", "row", None),
        P("lag", None, "row"),
        P(None, None, "row"),
        P("row", None, None),
    )
    out_specs = P(None, "lag", "row")

    return jax.shard_map(
        per_device, mesh=mesh, in_specs=in_specs, out_specs=out_specs, check_vma=False
    )
```

profile of v0, /device:TPU:0, one launch (start us, length us, event | category | flops | bytes accessed | tf_op | source)
XLA Modules:
  0.0 213.7 jit_solution(5984003146280783316)
XLA Ops:
  0.0 2.4 %slice_bitcast_fusion = (bf16[128,2048]{1,0:T(8,128)(2,1)}, bf16[128,2048]{1,0:T(8,128)(2,1)}) fusion(bf16[1,256,2048]{2,1,0:T(8,128)(2,1)} %param.5), kind=kLoop, calls=%fused_computation.5 | loop fusion | bytes 2097152 | tf_op jit(solution)/shard_map/slice | solution.py:102
  2.4 5.8 %collective-permute-start = (bf16[128,2048]{1,0:T(8,128)(2,1)}, bf16[128,2048]{1,0:T(8,128)(2,1)}, u32[]{:S(2)}, u32[]{:S(2)}) collective-permute-start(bf16[128,2048]{1,0:T(8,128)(2,1)} %get-tuple-element.28), channel_id=1, source_target_pairs={{0,1},{1,2},{2,3},{4,5},{5,6},{6,7},{8,9},{9,10},{10,11},{12,13},{... | collective-permute-start | bytes 1572872 | tf_op jit(solution)/shard_map/ppermute | solution.py:108
  9.5 5.3 %collective-permute-start.5 = (bf16[128,2048]{1,0:T(8,128)(2,1)}, bf16[128,2048]{1,0:T(8,128)(2,1)}, u32[]{:S(2)}, u32[]{:S(2)}) collective-permute-start(bf16[128,2048]{1,0:T(8,128)(2,1)} %get-tuple-element.27), channel_id=1, source_target_pairs={{0,1},{1,2},{2,3},{4,5},{5,6},{6,7},{8,9},{9,10},{10,11},{12,13},{... | collective-permute-start | bytes 1572872 | tf_op jit(solution)/shard_map/ppermute | solution.py:108
  17.9 12.2 %collective-permute-done.5 = bf16[128,2048]{1,0:T(8,128)(2,1)} collective-permute-done((bf16[128,2048]{1,0:T(8,128)(2,1)}, bf16[128,2048]{1,0:T(8,128)(2,1)}, u32[]{:S(2)}, u32[]{:S(2)}) %collective-permute-start.5) | collective-permute-done | bytes 524320 | tf_op jit(solution)/shard_map/ppermute | solution.py:108
  30.8 4.2 %collective-permute-done.7 = bf16[128,2048]{1,0:T(8,128)(2,1)} collective-permute-done((bf16[128,2048]{1,0:T(8,128)(2,1)}, bf16[128,2048]{1,0:T(8,128)(2,1)}, u32[]{:S(2)}, u32[]{:S(2)}) %collective-permute-start.7) | collective-permute-done | bytes 524320 | tf_op jit(solution)/shard_map/ppermute | solution.py:108
  43.4 8.5 %collective-permute-done.8 = bf16[128,2048]{1,0:T(8,128)(2,1)S(1)} collective-permute-done((bf16[128,2048]{1,0:T(8,128)(2,1)}, bf16[128,2048]{1,0:T(8,128)(2,1)S(1)}, u32[]{:S(2)}, u32[]{:S(2)}) %collective-permute-start.8) | collective-permute-done | bytes 524320 | tf_op jit(solution)/shard_map/ppermute | solution.py:108
  54.7 7.1 %collective-permute-done.3 = bf16[128,2048]{1,0:T(8,128)(2,1)S(1)} collective-permute-done((bf16[128,2048]{1,0:T(8,128)(2,1)}, bf16[128,2048]{1,0:T(8,128)(2,1)S(1)}, u32[]{:S(2)}, u32[]{:S(2)}) %collective-permute-start.3) | collective-permute-done | bytes 524320 | tf_op jit(solution)/shard_map/ppermute | solution.py:108
  64.6 7.7 %shard_map.46 = (f32[2,256,1024]{2,1,0:T(8,128)S(1)}, f32[2,256,1024]{2,1,0:T(8,128)S(1)}) custom-call(s32[3]{0:T(128)S(1)} %pad_add_fusion.4.idx, bf16[256,2048]{1,0:T(8,128)(2,1)S(1)} %bitcast.110, bf16[256,2048]{1,0:T(8,128)(2,1)S(1)} %collective-permute-done.13.refs_1_, bf16[2048,8192]{1,0:T(8,128)(2,1)} %bitcast.111), custom_call_target="tpu_custom_call" | custom-call | flops 4294967296 | bytes 16777216 | tf_op jit(solution)/shard_map/pallas_call | solution.py:72
  72.3 4.2 %shard_map.47 = (f32[2,256,1024]{2,1,0:T(8,128)S(1)}, f32[2,256,1024]{2,1,0:T(8,128)S(1)}) custom-call(s32[3]{0:T(128)S(1)} %pad_add_fusion.3.idx, bf16[256,2048]{1,0:T(8,128)(2,1)S(1)} %constant_dynamic-update-slice_fusion.2.refs_0_, bf16[256,2048]{1,0:T(8,128)(2,1)S(1)} %collective-permute-done.12.refs_1_, bf16[2048,8192]{1,0:T(8,128)(2,1)} %bitcast.112, ...), custom_call_target="tpu_custom_call" | custom-call | flops 4294967296 | bytes 16777216 | tf_op jit(solution)/shard_map/pallas_call | solution.py:72
  76.5 7.7 %shard_map.48 = (f32[2,256,1024]{2,1,0:T(8,128)S(1)}, f32[2,256,1024]{2,1,0:T(8,128)S(1)}) custom-call(s32[3]{0:T(128)S(1)} %pad_add_fusion.2.idx, bf16[256,2048]{1,0:T(8,128)(2,1)S(1)} %constant_dynamic-update-slice_fusion.refs_0_, bf16[256,2048]{1,0:T(8,128)(2,1)S(1)} %collective-permute-done.11.refs_1_, bf16[2048,8192]{1,0:T(8,128)(2,1)} %bitcast.113, ...), custom_call_target="tpu_custom_call" | custom-call | flops 4294967296 | bytes 16777216 | tf_op jit(solution)/shard_map/pallas_call | solution.py:72
  84.2 7.7 %shard_map.49 = (f32[2,256,1024]{2,1,0:T(8,128)S(1)}, f32[2,256,1024]{2,1,0:T(8,128)S(1)}) custom-call(s32[3]{0:T(128)S(1)} %pad_add_fusion.1.idx, bf16[256,2048]{1,0:T(8,128)(2,1)S(1)} %pad_maximum_fusion.refs_0_, bf16[256,2048]{1,0:T(8,128)(2,1)S(1)} %collective-permute-done.10.refs_1_, bf16[2048,8192]{1,0:T(8,128)(2,1)} %bitcast.114, ...), custom_call_target="tpu_custom_call" | custom-call | flops 4294967296 | bytes 16777216 | tf_op jit(solution)/shard_map/pallas_call | solution.py:72
  91.9 5.8 %shard_map.51 = f32[1,256,1024]{2,1,0:T(8,128)} custom-call(s32[3]{0:T(128)S(1)} %pad_add_fusion.idx, bf16[128,2048]{1,0:T(8,128)(2,1)S(1)} %collective-permute-done.4.refs_0_, bf16[128,2048]{1,0:T(8,128)(2,1)S(1)} %collective-permute-done.9.refs_1_, bf16[2048,8192]{1,0:T(8,128)(2,1)} %bitcast.115, f32[2,256,1024]{2,1,0:T(8,128)S(1)} %get-tuple-element.19.refs_3_), custom_call_target="tpu_custom_call" | custom-call | flops 1073741824 | bytes 6291456 | tf_op jit(solution)/shard_map/pallas_call | solution.py:72
  97.7 2.2 %collective-permute-start.14 = (f32[1,256,1024]{2,1,0:T(8,128)}, f32[1,256,1024]{2,1,0:T(8,128)}, u32[]{:S(2)}, u32[]{:S(2)}) collective-permute-start(f32[1,256,1024]{2,1,0:T(8,128)} %shard_map.51), channel_id=1, source_target_pairs={{0,4},{4,0},{8,12},{12,8},{16,20},{20,16},{24,28},{28,24},{1,5},{5... | collective-permute-start | bytes 3145736 | tf_op jit(solution)/shard_map/ppermute | solution.py:159
  102.0 4.1 %shard_map.50 = f32[1,256,1024]{2,1,0:T(8,128)S(1)} custom-call(s32[3]{0:T(128)S(1)} %pad_add_fusion.idx, bf16[128,2048]{1,0:T(8,128)(2,1)S(1)} %copy-done.6, bf16[128,2048]{1,0:T(8,128)(2,1)S(1)} %copy-done.3, bf16[2048,8192]{1,0:T(8,128)(2,1)} %bitcast.116, f32[2,256,1024]{2,1,0:T(8,128)S(1)} %get-tuple-element.19.refs_3_), custom_call_target="tpu_custom_call" | custom-call | flops 1073741824 | bytes 6291456 | tf_op jit(solution)/shard_map/pallas_call | solution.py:72
  112.8 5.0 %collective-permute-done.15 = f32[64,1024]{1,0:T(8,128)S(1)} collective-permute-done((f32[64,1024]{1,0:T(8,128)}, f32[64,1024]{1,0:T(8,128)S(1)}, u32[]{:S(2)}, u32[]{:S(2)}) %collective-permute-start.15) | collective-permute-done | bytes 262176 | tf_op jit(solution)/shard_map/ppermute | solution.py:168
  117.8 5.3 %collective-permute-done.16 = f32[64,1024]{1,0:T(8,128)} collective-permute-done((f32[64,1024]{1,0:T(8,128)}, f32[64,1024]{1,0:T(8,128)}, u32[]{:S(2)}, u32[]{:S(2)}) %collective-permute-start.16) | collective-permute-done | bytes 262176 | tf_op jit(solution)/shard_map/ppermute | solution.py:168
  125.0 2.2 %fusion = bf16[8,8,8,128]{3,2,1,0:T(8,128)(2,1)S(1)} fusion(f32[16,128,128]{2,1,0:T(8,128)S(1)} %copy-done, s32[]{:T(128)S(6)} %select_n.93, f32[2,256,2048]{2,1,0:T(8,128)} %param.6, s32[]{:T(128)S(6)} %select_n.82, s32[]{:T(128)S(6)} %select_n.83, f32[64,1024]{1,0:T(8,128)} %collective-permute-done.17, f32[64,1024]{1,0:T(8,128)} %collective-permute-done.16, ...), kind=kOutput, calls=%fused_computation.2 | convolution fusion | flops 100990976 | bytes 1966096 | tf_op jit(solution)/shard_map/bij,rbj->rbi/dot_general | solution.py:96
  127.3 2.4 %collective-permute-start.35 = (bf16[128,2048]{1,0:T(8,128)(2,1)S(1)}, bf16[128,2048]{1,0:T(8,128)(2,1)S(1)}, u32[]{:S(2)}, u32[]{:S(2)}) collective-permute-start(bf16[128,2048]{1,0:T(8,128)(2,1)S(1)} %copy-done.4), channel_id=1, source_target_pairs={{3,7},{0,4},{7,11},{4,8},{11,15},{8,12},{15,19},{12,16},{19,23},{1... | collective-permute-start | bytes 1572872 | tf_op jit(solution)/shard_map/ppermute | solution.py:155
  133.3 2.5 %collective-permute-start.28 = (bf16[64,2048]{1,0:T(8,128)(2,1)S(1)}, bf16[64,2048]{1,0:T(8,128)(2,1)}, u32[]{:S(2)}, u32[]{:S(2)}) collective-permute-start(bf16[64,2048]{1,0:T(8,128)(2,1)S(1)} %pad_maximum_fusion.1.refs_0_), channel_id=1, source_target_pairs={{0,1},{1,0},{2,3},{3,2},{8,9},{9,8},{10,11},{11,10},{16,17},{17,16... | collective-permute-start | bytes 786440 | tf_op jit(solution)/shard_map/ppermute | solution.py:197
  141.3 5.0 %collective-permute-start.19 = (bf16[64,2048]{1,0:T(8,128)(2,1)S(1)}, bf16[64,2048]{1,0:T(8,128)(2,1)S(1)}, u32[]{:S(2)}, u32[]{:S(2)}) collective-permute-start(bf16[64,2048]{1,0:T(8,128)(2,1)S(1)} %pad_maximum_fusion.1.refs_0_), channel_id=1, source_target_pairs={{0,3},{1,2},{2,1},{3,0},{8,11},{9,10},{10,9},{11,8},{16,19},{17,18... | collective-permute-start | bytes 786440 | tf_op jit(solution)/shard_map/ppermute | solution.py:197
  150.9 2.4 %collective-permute-done.24.refs_0_ = bf16[64,2048]{1,0:T(8,128)(2,1)S(1)} collective-permute-done((bf16[64,2048]{1,0:T(8,128)(2,1)S(1)}, bf16[64,2048]{1,0:T(8,128)(2,1)S(1)}, u32[]{:S(2)}, u32[]{:S(2)}) %collective-permute-start.24) | collective-permute-done | bytes 262176 | tf_op jit(solution)/shard_map/ppermute | solution.py:197
  156.1 5.4 %shard_map.52.refs_5_ = f32[2,256,1024]{2,1,0:T(8,128)S(1)} custom-call(s32[3]{0:T(128)S(1)} %pad_add_fusion.idx, bf16[128,2048]{1,0:T(8,128)(2,1)S(1)} %collective-permute-done.34.refs_0_, bf16[128,2048]{1,0:T(8,128)(2,1)S(1)} %collective-permute-done.35.refs_1_, bf16[2048,8192]{1,0:T(8,128)(2,1)} %bitcast.117, f32[2,256,1024]{2,1,0:T(8,128)S(1)} %copy-done.9), custom_call_target="tpu_custom_call" | custom-call | flops 2147483648 | bytes 12582912 | tf_op jit(solution)/shard_map/pallas_call | solution.py:72
  164.8 5.6 %shard_map.53.refs_5_ = f32[2,256,1024]{2,1,0:T(8,128)S(1)} custom-call(s32[3]{0:T(128)S(1)} %pad_add_fusion.6.idx, bf16[64,2048]{1,0:T(8,128)(2,1)S(1)} %pad_maximum_fusion.1.refs_0_, bf16[64,2048]{1,0:T(8,128)(2,1)} %collective-permute-done.32.refs_1_, bf16[64,2048]{1,0:T(8,128)(2,1)S(1)} %collective-permute-done.33.refs_2_, ...), custom_call_target="tpu_custom_call" | custom-call | flops 2147483648 | bytes 12582912 | tf_op jit(solution)/shard_map/pallas_call | solution.py:72
  173.1 2.6 %collective-permute-start.23 = (bf16[64,2048]{1,0:T(8,128)(2,1)}, bf16[64,2048]{1,0:T(8,128)(2,1)S(1)}, u32[]{:S(2)}, u32[]{:S(2)}) collective-permute-start(bf16[64,2048]{1,0:T(8,128)(2,1)} %collective-permute-done.22.refs_3_), channel_id=1, source_target_pairs={{0,3},{1,2},{2,1},{3,0}} | collective-permute-start | bytes 786440 | tf_op jit(solution)/shard_map/ppermute | solution.py:197
  175.7 5.5 %shard_map.54.refs_5_ = f32[2,256,1024]{2,1,0:T(8,128)S(1)} custom-call(s32[3]{0:T(128)S(1)} %add_add_fusion.2.idx, bf16[64,2048]{1,0:T(8,128)(2,1)} %collective-permute-done.28.refs_0_, bf16[64,2048]{1,0:T(8,128)(2,1)S(1)} %collective-permute-done.29.refs_1_, bf16[64,2048]{1,0:T(8,128)(2,1)S(1)} %collective-permute-done.30.refs_2_, ...), custom_call_target="tpu_custom_call" | custom-call | flops 2147483648 | bytes 12582912 | tf_op jit(solution)/shard_map/pallas_call | solution.py:72
  181.2 5.4 %shard_map.55.refs_5_ = f32[2,256,1024]{2,1,0:T(8,128)S(1)} custom-call(s32[3]{0:T(128)S(1)} %add_add_fusion.1.idx, bf16[64,2048]{1,0:T(8,128)(2,1)S(1)} %collective-permute-done.24.refs_0_, bf16[64,2048]{1,0:T(8,128)(2,1)S(1)} %collective-permute-done.25.refs_1_, bf16[64,2048]{1,0:T(8,128)(2,1)S(1)} %collective-permute-done.26.refs_2_, ...), custom_call_target="tpu_custom_call" | custom-call | flops 2147483648 | bytes 12582912 | tf_op jit(solution)/shard_map/pallas_call | solution.py:72
  186.7 4.1 %shard_map.57 = f32[1,256,1024]{2,1,0:T(8,128)S(1)} custom-call(s32[3]{0:T(128)S(1)} %add_add_fusion.idx, bf16[64,2048]{1,0:T(8,128)(2,1)S(1)} %collective-permute-done.19.refs_0_, bf16[64,2048]{1,0:T(8,128)(2,1)S(1)} %collective-permute-done.20.refs_1_, bf16[64,2048]{1,0:T(8,128)(2,1)S(1)} %collective-permute-done.21.refs_2_, ...), custom_call_target="tpu_custom_call" | custom-call | flops 1073741824 | bytes 6291456 | tf_op jit(solution)/shard_map/pallas_call | solution.py:72
  190.9 4.3 %shard_map.56 = f32[1,256,1024]{2,1,0:T(8,128)S(1)} custom-call(s32[3]{0:T(128)S(1)} %add_add_fusion.idx, bf16[64,2048]{1,0:T(8,128)(2,1)S(1)} %collective-permute-done.19.refs_0_, bf16[64,2048]{1,0:T(8,128)(2,1)S(1)} %collective-permute-done.20.refs_1_, bf16[64,2048]{1,0:T(8,128)(2,1)S(1)} %collective-permute-done.21.refs_2_, ...), custom_call_target="tpu_custom_call" | custom-call | flops 1073741824 | bytes 6291456 | tf_op jit(solution)/shard_map/pallas_call | solution.py:72
  196.2 3.5 %collective-permute-start.39 = (f32[64,1024]{1,0:T(8,128)S(1)}, f32[64,1024]{1,0:T(8,128)}, u32[]{:S(2)}, u32[]{:S(2)}) collective-permute-start(f32[64,1024]{1,0:T(8,128)S(1)} %get-tuple-element.22), channel_id=1, source_target_pairs={{0,24},{4,28},{8,16},{12,20},{16,8},{20,12},{24,0},{28,4},{1,25},{... | collective-permute-start | bytes 786440 | tf_op jit(solution)/shard_map/ppermute | solution.py:168
  199.7 5.9 %collective-permute-done.37 = f32[64,1024]{1,0:T(8,128)S(1)} collective-permute-done((f32[64,1024]{1,0:T(8,128)}, f32[64,1024]{1,0:T(8,128)S(1)}, u32[]{:S(2)}, u32[]{:S(2)}) %collective-permute-start.37) | collective-permute-done | bytes 262176 | tf_op jit(solution)/shard_map/ppermute | solution.py:168
  205.6 3.7 %collective-permute-done.38 = f32[64,1024]{1,0:T(8,128)S(1)} collective-permute-done((f32[64,1024]{1,0:T(8,128)S(1)}, f32[64,1024]{1,0:T(8,128)S(1)}, u32[]{:S(2)}, u32[]{:S(2)}) %collective-permute-start.38) | collective-permute-done | bytes 262176 | tf_op jit(solution)/shard_map/ppermute | solution.py:168
  209.3 2.1 %fusion.1 = bf16[8,8,8,128]{3,2,1,0:T(8,128)(2,1)S(1)} fusion(f32[16,128,128]{2,1,0:T(8,128)S(1)} %copy-done, s32[]{:T(128)S(6)} %select_n.93, f32[2,256,2048]{2,1,0:T(8,128)} %param.6, s32[]{:T(128)S(6)} %add.112, s32[]{:T(128)S(6)} %select_n.82, s32[]{:T(128)S(6)} %select_n.83, f32[64,1024]{1,0:T(8,128)} %collective-permute-done.39, ...), kind=kOutput, calls=%fused_computation.3 | convolution fusion | flops 100990976 | bytes 1966100 | tf_op jit(solution)/shard_map/bij,rbj->rbi/dot_general | solution.py:96
  (121 shorter events, 54.8 us)
Async XLA Ops:
  2.4 33.9 %collective-permute-start = (bf16[128,2048]{1,0:T(8,128)(2,1)}, bf16[128,2048]{1,0:T(8,128)(2,1)}, u32[]{:S(2)}, u32[]{:S(2)}) collective-permute-start(bf16[128,2048]{1,0:T(8,128)(2,1)} %get-tuple-element.28), channel_id=1, source_target_pairs={{0,1},{1,2},{2,3},{4,5},{5,6},{6,7},{8,9},{9,10},{10,11},{12,13},{... | collective-permute-start | bytes 1572872 | tf_op jit(solution)/shard_map/ppermute | solution.py:108
  8.2 29.9 %collective-permute-start.2 = (bf16[128,2048]{1,0:T(8,128)(2,1)}, bf16[128,2048]{1,0:T(8,128)(2,1)}, u32[]{:S(2)}, u32[]{:S(2)}) collective-permute-start(bf16[128,2048]{1,0:T(8,128)(2,1)} %get-tuple-element.28), channel_id=1, source_target_pairs={{1,0},{2,1},{3,2},{5,4},{6,5},{7,6},{9,8},{10,9},{11,10},{13,12},{... | collective-permute-start | bytes 1572872 | tf_op jit(solution)/shard_map/ppermute | solution.py:108
  9.5 20.6 %collective-permute-start.5 = (bf16[128,2048]{1,0:T(8,128)(2,1)}, bf16[128,2048]{1,0:T(8,128)(2,1)}, u32[]{:S(2)}, u32[]{:S(2)}) collective-permute-start(bf16[128,2048]{1,0:T(8,128)(2,1)} %get-tuple-element.27), channel_id=1, source_target_pairs={{0,1},{1,2},{2,3},{4,5},{5,6},{6,7},{8,9},{9,10},{10,11},{12,13},{... | collective-permute-start | bytes 1572872 | tf_op jit(solution)/shard_map/ppermute | solution.py:108
  14.9 20.2 %collective-permute-start.7 = (bf16[128,2048]{1,0:T(8,128)(2,1)}, bf16[128,2048]{1,0:T(8,128)(2,1)}, u32[]{:S(2)}, u32[]{:S(2)}) collective-permute-start(bf16[128,2048]{1,0:T(8,128)(2,1)} %get-tuple-element.27), channel_id=1, source_target_pairs={{1,0},{2,1},{3,2},{5,4},{6,5},{7,6},{9,8},{10,9},{11,10},{13,12},{... | collective-permute-start | bytes 1572872 | tf_op jit(solution)/shard_map/ppermute | solution.py:108
  16.2 47.1 %collective-permute-start.13 = (bf16[256,2048]{1,0:T(8,128)(2,1)S(1)}, bf16[256,2048]{1,0:T(8,128)(2,1)S(1)}, u32[]{:S(2)}, u32[]{:S(2)}) collective-permute-start(bf16[256,2048]{1,0:T(8,128)(2,1)S(1)} %bitcast.109), channel_id=1, source_target_pairs={{0,4},{1,5},{2,6},{3,7},{4,8},{5,9},{6,10},{7,11},{8,12},{9,13},{1... | collective-permute-start | bytes 3145736 | tf_op jit(solution)/shard_map/ppermute | solution.py:155
  30.1 12.6 %collective-permute-start.6 = (bf16[128,2048]{1,0:T(8,128)(2,1)}, bf16[128,2048]{1,0:T(8,128)(2,1)S(1)}, u32[]{:S(2)}, u32[]{:S(2)}) collective-permute-start(bf16[128,2048]{1,0:T(8,128)(2,1)} %collective-permute-done.5), channel_id=1, source_target_pairs={{1,2},{2,3},{5,6},{6,7},{9,10},{10,11},{13,14},{14,15},{17,18},{18... | collective-permute-start | bytes 1572872 | tf_op jit(solution)/shard_map/ppermute | solution.py:108
  35.0 16.9 %collective-permute-start.8 = (bf16[128,2048]{1,0:T(8,128)(2,1)}, bf16[128,2048]{1,0:T(8,128)(2,1)S(1)}, u32[]{:S(2)}, u32[]{:S(2)}) collective-permute-start(bf16[128,2048]{1,0:T(8,128)(2,1)} %collective-permute-done.7), channel_id=1, source_target_pairs={{1,0},{2,1},{5,4},{6,5},{9,8},{10,9},{13,12},{14,13},{17,16},{18,1... | collective-permute-start | bytes 1572872 | tf_op jit(solution)/shard_map/ppermute | solution.py:108
  36.3 17.0 %collective-permute-start.1 = (bf16[128,2048]{1,0:T(8,128)(2,1)}, bf16[128,2048]{1,0:T(8,128)(2,1)S(1)}, u32[]{:S(2)}, u32[]{:S(2)}) collective-permute-start(bf16[128,2048]{1,0:T(8,128)(2,1)} %collective-permute-done), channel_id=1, source_target_pairs={{1,2},{2,3},{5,6},{6,7},{9,10},{10,11},{13,14},{14,15},{17,18},{18... | collective-permute-start | bytes 1572872 | tf_op jit(solution)/shard_map/ppermute | solution.py:108
  39.2 22.6 %collective-permute-start.3 = (bf16[128,2048]{1,0:T(8,128)(2,1)}, bf16[128,2048]{1,0:T(8,128)(2,1)S(1)}, u32[]{:S(2)}, u32[]{:S(2)}) collective-permute-start(bf16[128,2048]{1,0:T(8,128)(2,1)} %collective-permute-done.2), channel_id=1, source_target_pairs={{1,0},{2,1},{5,4},{6,5},{9,8},{10,9},{13,12},{14,13},{17,16},{18,1... | collective-permute-start | bytes 1572872 | tf_op jit(solution)/shard_map/ppermute | solution.py:108
  42.7 29.6 %collective-permute-start.12 = (bf16[256,2048]{1,0:T(8,128)(2,1)S(1)}, bf16[256,2048]{1,0:T(8,128)(2,1)S(1)}, u32[]{:S(2)}, u32[]{:S(2)}) collective-permute-start(bf16[256,2048]{1,0:T(8,128)(2,1)S(1)} %constant_dynamic-update-slice_fusion.2.refs_0_), channel_id=1, source_target_pairs={{1,5},{2,6},{3,7},{5,9},{6,10},{7,11},{9,13},{10,14},{11,15},{13,1... | collective-permute-start | bytes 3145736 | tf_op jit(solution)/shard_map/ppermute | solution.py:155
  51.9 24.6 %collective-permute-start.11 = (bf16[256,2048]{1,0:T(8,128)(2,1)S(1)}, bf16[256,2048]{1,0:T(8,128)(2,1)S(1)}, u32[]{:S(2)}, u32[]{:S(2)}) collective-permute-start(bf16[256,2048]{1,0:T(8,128)(2,1)S(1)} %constant_dynamic-update-slice_fusion.refs_0_), channel_id=1, source_target_pairs={{0,4},{1,5},{2,6},{4,8},{5,9},{6,10},{8,12},{9,13},{10,14},{12,16}... | collective-permute-start | bytes 3145736 | tf_op jit(solution)/shard_map/ppermute | solution.py:155
  53.4 38.6 %collective-permute-start.9 = (bf16[128,2048]{1,0:T(8,128)(2,1)S(1)}, bf16[128,2048]{1,0:T(8,128)(2,1)S(1)}, u32[]{:S(2)}, u32[]{:S(2)}) collective-permute-start(bf16[128,2048]{1,0:T(8,128)(2,1)S(1)} %broadcast_select_fusion), channel_id=1, source_target_pairs={{2,3},{1,0},{6,7},{5,4},{10,11},{9,8},{14,15},{13,12},{18,19},{17,... | collective-permute-start | bytes 1572872 | tf_op jit(solution)/shard_map/ppermute | solution.py:108
  61.8 30.1 %collective-permute-start.4 = (bf16[128,2048]{1,0:T(8,128)(2,1)S(1)}, bf16[128,2048]{1,0:T(8,128)(2,1)S(1)}, u32[]{:S(2)}, u32[]{:S(2)}) collective-permute-start(bf16[128,2048]{1,0:T(8,128)(2,1)S(1)} %broadcast_select_fusion.1), channel_id=1, source_target_pairs={{2,3},{1,0},{6,7},{5,4},{10,11},{9,8},{14,15},{13,12},{18,19},{17,... | collective-permute-start | bytes 1572872 | tf_op jit(solution)/shard_map/ppermute | solution.py:108
  63.3 20.9 %collective-permute-start.10 = (bf16[256,2048]{1,0:T(8,128)(2,1)S(1)}, bf16[256,2048]{1,0:T(8,128)(2,1)S(1)}, u32[]{:S(2)}, u32[]{:S(2)}) collective-permute-start(bf16[256,2048]{1,0:T(8,128)(2,1)S(1)} %pad_maximum_fusion.refs_0_), channel_id=1, source_target_pairs={{2,6},{3,7},{0,4},{1,5},{6,10},{7,11},{4,8},{5,9},{10,14},{11,15},... | collective-permute-start | bytes 3145736 | tf_op jit(solution)/shard_map/ppermute | solution.py:155
  109.9 13.2 %collective-permute-start.16 = (f32[64,1024]{1,0:T(8,128)}, f32[64,1024]{1,0:T(8,128)}, u32[]{:S(2)}, u32[]{:S(2)}) collective-permute-start(f32[64,1024]{1,0:T(8,128)} %get-tuple-element.26), channel_id=1, source_target_pairs={{0,16},{4,20},{8,24},{12,28},{16,0},{20,4},{24,8},{28,12},{1,17},{... | collective-permute-start | bytes 786440 | tf_op jit(solution)/shard_map/ppermute | solution.py:168
  111.3 13.6 %collective-permute-start.17 = (f32[64,1024]{1,0:T(8,128)}, f32[64,1024]{1,0:T(8,128)}, u32[]{:S(2)}, u32[]{:S(2)}) collective-permute-start(f32[64,1024]{1,0:T(8,128)} %get-tuple-element.25), channel_id=1, source_target_pairs={{0,24},{4,28},{8,16},{12,20},{16,8},{20,12},{24,0},{28,4},{1,25},{... | collective-permute-start | bytes 786440 | tf_op jit(solution)/shard_map/ppermute | solution.py:168
  133.3 13.0 %collective-permute-start.28 = (bf16[64,2048]{1,0:T(8,128)(2,1)S(1)}, bf16[64,2048]{1,0:T(8,128)(2,1)}, u32[]{:S(2)}, u32[]{:S(2)}) collective-permute-start(bf16[64,2048]{1,0:T(8,128)(2,1)S(1)} %pad_maximum_fusion.1.refs_0_), channel_id=1, source_target_pairs={{0,1},{1,0},{2,3},{3,2},{8,9},{9,8},{10,11},{11,10},{16,17},{17,16... | collective-permute-start | bytes 786440 | tf_op jit(solution)/shard_map/ppermute | solution.py:197
  135.9 11.8 %collective-permute-start.32 = (bf16[64,2048]{1,0:T(8,128)(2,1)S(1)}, bf16[64,2048]{1,0:T(8,128)(2,1)}, u32[]{:S(2)}, u32[]{:S(2)}) collective-permute-start(bf16[64,2048]{1,0:T(8,128)(2,1)S(1)} %pad_maximum_fusion.1.refs_0_), channel_id=1, source_target_pairs={{8,0},{9,1},{10,2},{11,3}} | collective-permute-start | bytes 786440 | tf_op jit(solution)/shard_map/ppermute | solution.py:193
  137.2 11.8 %collective-permute-start.33 = (bf16[64,2048]{1,0:T(8,128)(2,1)S(1)}, bf16[64,2048]{1,0:T(8,128)(2,1)S(1)}, u32[]{:S(2)}, u32[]{:S(2)}) collective-permute-start(bf16[64,2048]{1,0:T(8,128)(2,1)S(1)} %pad_maximum_fusion.1.refs_0_), channel_id=1, source_target_pairs={{16,0},{17,1},{18,2},{19,3}} | collective-permute-start | bytes 786440 | tf_op jit(solution)/shard_map/ppermute | solution.py:193
  138.5 14.8 %collective-permute-start.24 = (bf16[64,2048]{1,0:T(8,128)(2,1)S(1)}, bf16[64,2048]{1,0:T(8,128)(2,1)S(1)}, u32[]{:S(2)}, u32[]{:S(2)}) collective-permute-start(bf16[64,2048]{1,0:T(8,128)(2,1)S(1)} %pad_maximum_fusion.1.refs_0_), channel_id=1, source_target_pairs={{0,2},{1,3},{2,0},{3,1},{8,10},{9,11},{10,8},{11,9},{16,18},{17,19... | collective-permute-start | bytes 786440 | tf_op jit(solution)/shard_map/ppermute | solution.py:197
  141.3 20.3 %collective-permute-start.19 = (bf16[64,2048]{1,0:T(8,128)(2,1)S(1)}, bf16[64,2048]{1,0:T(8,128)(2,1)S(1)}, u32[]{:S(2)}, u32[]{:S(2)}) collective-permute-start(bf16[64,2048]{1,0:T(8,128)(2,1)S(1)} %pad_maximum_fusion.1.refs_0_), channel_id=1, source_target_pairs={{0,3},{1,2},{2,1},{3,0},{8,11},{9,10},{10,9},{11,8},{16,19},{17,18... | collective-permute-start | bytes 786440 | tf_op jit(solution)/shard_map/ppermute | solution.py:197
  146.3 16.6 %collective-permute-start.29 = (bf16[64,2048]{1,0:T(8,128)(2,1)}, bf16[64,2048]{1,0:T(8,128)(2,1)S(1)}, u32[]{:S(2)}, u32[]{:S(2)}) collective-permute-start(bf16[64,2048]{1,0:T(8,128)(2,1)} %collective-permute-done.28.refs_0_), channel_id=1, source_target_pairs={{8,0},{9,1},{10,2},{11,3}} | collective-permute-start | bytes 786440 | tf_op jit(solution)/shard_map/ppermute | solution.py:193
  147.7 22.8 %collective-permute-start.30 = (bf16[64,2048]{1,0:T(8,128)(2,1)}, bf16[64,2048]{1,0:T(8,128)(2,1)S(1)}, u32[]{:S(2)}, u32[]{:S(2)}) collective-permute-start(bf16[64,2048]{1,0:T(8,128)(2,1)} %collective-permute-done.28.refs_0_), channel_id=1, source_target_pairs={{16,0},{17,1},{18,2},{19,3}} | collective-permute-start | bytes 786440 | tf_op jit(solution)/shard_map/ppermute | solution.py:193
  149.0 22.8 %collective-permute-start.31 = (bf16[64,2048]{1,0:T(8,128)(2,1)}, bf16[64,2048]{1,0:T(8,128)(2,1)S(1)}, u32[]{:S(2)}, u32[]{:S(2)}) collective-permute-start(bf16[64,2048]{1,0:T(8,128)(2,1)} %collective-permute-done.22.refs_3_), channel_id=1, source_target_pairs={{0,1},{1,0},{2,3},{3,2}} | collective-permute-start | bytes 786440 | tf_op jit(solution)/shard_map/ppermute | solution.py:197
  153.3 19.8 %collective-permute-start.25 = (bf16[64,2048]{1,0:T(8,128)(2,1)S(1)}, bf16[64,2048]{1,0:T(8,128)(2,1)S(1)}, u32[]{:S(2)}, u32[]{:S(2)}) collective-permute-start(bf16[64,2048]{1,0:T(8,128)(2,1)S(1)} %collective-permute-done.24.refs_0_), channel_id=1, source_target_pairs={{8,0},{9,1},{10,2},{11,3}} | collective-permute-start | bytes 786440 | tf_op jit(solution)/shard_map/ppermute | solution.py:193
  161.6 19.6 %collective-permute-start.26 = (bf16[64,2048]{1,0:T(8,128)(2,1)S(1)}, bf16[64,2048]{1,0:T(8,128)(2,1)S(1)}, u32[]{:S(2)}, u32[]{:S(2)}) collective-permute-start(bf16[64,2048]{1,0:T(8,128)(2,1)S(1)} %collective-permute-done.24.refs_0_), channel_id=1, source_target_pairs={{16,0},{17,1},{18,2},{19,3}} | collective-permute-start | bytes 786440 | tf_op jit(solution)/shard_map/ppermute | solution.py:193
  162.9 18.3 %collective-permute-start.27 = (bf16[64,2048]{1,0:T(8,128)(2,1)}, bf16[64,2048]{1,0:T(8,128)(2,1)S(1)}, u32[]{:S(2)}, u32[]{:S(2)}) collective-permute-start(bf16[64,2048]{1,0:T(8,128)(2,1)} %collective-permute-done.22.refs_3_), channel_id=1, source_target_pairs={{0,2},{1,3},{2,0},{3,1}} | collective-permute-start | bytes 786440 | tf_op jit(solution)/shard_map/ppermute | solution.py:197
  170.4 16.2 %collective-permute-start.20 = (bf16[64,2048]{1,0:T(8,128)(2,1)S(1)}, bf16[64,2048]{1,0:T(8,128)(2,1)S(1)}, u32[]{:S(2)}, u32[]{:S(2)}) collective-permute-start(bf16[64,2048]{1,0:T(8,128)(2,1)S(1)} %collective-permute-done.19.refs_0_), channel_id=1, source_target_pairs={{8,0},{9,1},{10,2},{11,3}} | collective-permute-start | bytes 786440 | tf_op jit(solution)/shard_map/ppermute | solution.py:193
  171.8 14.9 %collective-permute-start.21 = (bf16[64,2048]{1,0:T(8,128)(2,1)S(1)}, bf16[64,2048]{1,0:T(8,128)(2,1)S(1)}, u32[]{:S(2)}, u32[]{:S(2)}) collective-permute-start(bf16[64,2048]{1,0:T(8,128)(2,1)S(1)} %collective-permute-done.19.refs_0_), channel_id=1, source_target_pairs={{16,0},{17,1},{18,2},{19,3}} | collective-permute-start | bytes 786440 | tf_op jit(solution)/shard_map/ppermute | solution.py:193
  173.1 13.6 %collective-permute-start.23 = (bf16[64,2048]{1,0:T(8,128)(2,1)}, bf16[64,2048]{1,0:T(8,128)(2,1)S(1)}, u32[]{:S(2)}, u32[]{:S(2)}) collective-permute-start(bf16[64,2048]{1,0:T(8,128)(2,1)} %collective-permute-done.22.refs_3_), channel_id=1, source_target_pairs={{0,3},{1,2},{2,1},{3,0}} | collective-permute-start | bytes 786440 | tf_op jit(solution)/shard_map/ppermute | solution.py:197
  196.2 13.1 %collective-permute-start.38 = (f32[64,1024]{1,0:T(8,128)S(1)}, f32[64,1024]{1,0:T(8,128)S(1)}, u32[]{:S(2)}, u32[]{:S(2)}) collective-permute-start(f32[64,1024]{1,0:T(8,128)S(1)} %get-tuple-element.23), channel_id=1, source_target_pairs={{0,16},{4,20},{8,24},{12,28},{16,0},{20,4},{24,8},{28,12},{1,17},{... | collective-permute-start | bytes 786440 | tf_op jit(solution)/shard_map/ppermute | solution.py:168
  196.2 13.1 %collective-permute-start.39 = (f32[64,1024]{1,0:T(8,128)S(1)}, f32[64,1024]{1,0:T(8,128)}, u32[]{:S(2)}, u32[]{:S(2)}) collective-permute-start(f32[64,1024]{1,0:T(8,128)S(1)} %get-tuple-element.22), channel_id=1, source_target_pairs={{0,24},{4,28},{8,16},{12,20},{16,8},{20,12},{24,0},{28,4},{1,25},{... | collective-permute-start | bytes 786440 | tf_op jit(solution)/shard_map/ppermute | solution.py:168
  (23 other events, 309.7 us)
where the time goes:
time: 215 us; the launch traced here: 214 us
  Pallas kernels  67.4 us (31%)
  starting transfers between devices  67.3 us (31%)
  waiting for transfers between devices  58.2 us (27%)
  local copies, waits for them, and re-layouts  12.2 us (6%)
  matrix products  4.39 us (2%)
  other arithmetic  3.24 us (2%)
    pallas_call x12, Pallas kernels, product(): pl.pallas_call(functools.partial(product_kernel, count=count, groups=grou...  67.4 us
    ppermute x10, waiting for transfers between devices, send(): out.append(lax.ppermute(piece, 'row', pairs))  32.1 us
    ppermute x6, waiting for transfers between devices, reduce_chips(): total += lax.ppermute(sent, 'lag', [(i, i ^ 2 * d) for i in range(lags)])  21.8 us
    ppermute x10, starting transfers between devices, send(): out.append(lax.ppermute(piece, 'row', pairs))  20.2 us
    ppermute x6, starting transfers between devices, along(): return lax.ppermute(x, ('lag', 'row'), pairs)  15.9 us
    ppermute x9, starting transfers between devices, to_first(): return lax.ppermute(x, 'lag', [(2 * k, 0)])  11.6 us
    ppermute x6, starting transfers between devices, older(): return lax.ppermute(value, ('lag', 'row'), pairs)  9.32 us
    ppermute x6, starting transfers between devices, reduce_chips(): total += lax.ppermute(sent, 'lag', [(i, i ^ 2 * d) for i in range(lags)])  7.84 us
  transfers between devices with their start and end apart: 41, of which 12 were waited for; matrix products, arithmetic and copies ran while one was open for 2% of the time, Pallas kernels for 27%

commit v1 on v0

v1 whole, which is shorter than its diff:
```python
import functools

import jax
import jax.numpy as jnp
from jax import lax
from jax.experimental import pallas as pl
from jax.experimental.pallas import tpu as pltpu
from jax.sharding import PartitionSpec as P


def product_kernel(idx, *refs, count, groups, add, shared):
    xs, a_ref = refs[:count], refs[count]
    rest = list(refs[count + 1 :])
    b_ref = rest.pop(0) if shared else None
    c_refs = [rest.pop(0) for _ in range(groups)] if add else None
    o_refs = [rest.pop(0) for _ in range(groups)]
    buf = xs[0]
    if count > 1:
        buf = rest.pop(0)

        @pl.when(pl.program_id(0) == 0)
        def _():
            at = 0
            for x in xs:
                buf[at : at + x.shape[0]] = x[...]
                at += x.shape[0]

    def put(values):
        at = 0
        for k, o in enumerate(o_refs):
            rows = o.shape[1]
            if values is None:
                o[0] = c_refs[k][0]
            elif add:
                o[0] = c_refs[k][0] + values[at : at + rows]
            else:
                o[0] = values[at : at + rows]
            at += rows

    def value(ref):
        return lax.dot_general(
            buf[...], ref[...], (((1,), (1,)), ((), ())), preferred_element_type=jnp.float32
        )

    if not add:
        put(value(a_ref))
        return

    @pl.when(idx[2] == 1)
    def _():
        put(value(a_ref))

    if shared:

        @pl.when(idx[2] == 2)
        def _():
            put(value(b_ref))

    @pl.when(idx[2] == 0)
    def _():
        put(None)


def product(idx, xs, matrix, totals=None, side=None, groups=1, mates=None):
    places = [x if isinstance(x, tuple) else (x, None) for x in xs]
    count, width = len(xs), places[0][0].shape[-1]
    rows = sum(x.shape[-2] for x, _ in places)
    each = rows // groups
    half = matrix.shape[0] // 2
    first, steps = (0, 2) if side is None else (side, 1)
    in_specs, stacked = [], []
    for x, place in places:
        stacked.append(x)
        if place is None:
            in_specs.append(pl.BlockSpec(x.shape, lambda t, s: (0, 0)))
        else:
            in_specs.append(
                pl.BlockSpec((None, *x.shape[1:]), lambda t, s, place=place: (place, 0, 0))
            )
    tile = lambda t, s: (1 - s[1] + t + first) % 2
    operands = [*stacked, matrix]
    if mates is None:
        in_specs.append(pl.BlockSpec((half, width), lambda t, s: (tile(t, s), s[0])))
    else:
        keep = lambda want, s, x: jnp.where(s[2] == want, x, 0)
        in_specs.append(
            pl.BlockSpec((half, width), lambda t, s: (keep(1, s, tile(t, s)), keep(1, s, s[0])))
        )
        in_specs.append(
            pl.BlockSpec(
                (None, half, width), lambda t, s: (keep(2, s, s[3]), keep(2, s, tile(t, s)), 0)
            )
        )
        operands.append(mates)
    if totals is not None:
        in_specs += [pl.BlockSpec((1, each, half), lambda t, s: (t + first, 0, 0))] * groups
        operands += totals
    scratch = [pltpu.VMEM((rows, width), matrix.dtype)] if count > 1 else []
    return pl.pallas_call(
        functools.partial(
            product_kernel,
            count=count,
            groups=groups,
            add=totals is not None,
            shared=mates is not None,
        ),
        out_shape=[jax.ShapeDtypeStruct((steps, each, half), jnp.float32)] * groups,
        grid_spec=pltpu.PrefetchScalarGridSpec(
            num_scalar_prefetch=1,
            grid=(steps,),
            in_specs=in_specs,
            out_specs=[pl.BlockSpec((1, each, half), lambda t, s: (t, 0, 0))] * groups,
            scratch_shapes=scratch,
        ),
        compiler_params=pltpu.CompilerParams(
            dimension_semantics=("arbitrary",), vmem_limit_bytes=(32 if groups > 1 else 24) << 20
        ),
        cost_estimate=pl.CostEstimate(
            flops=2 * rows * steps * half * width,
            bytes_accessed=steps * half * (2 * width + 8 * rows),
            transcendentals=0,
        ),
    )(idx, *operands)


def copy_kernel(x_ref, o_ref):
    o_ref[0] = x_ref[...]


def second_halves(matrix, blocks):
    rows, half = matrix.shape[0], matrix.shape[1] // blocks // 2
    return pl.pallas_call(
        copy_kernel,
        out_shape=jax.ShapeDtypeStruct((blocks, rows, half), matrix.dtype),
        grid=(blocks, 2),
        in_specs=[pl.BlockSpec((rows // 2, half), lambda b, t: (t, 2 * b + 1))],
        out_specs=pl.BlockSpec((1, rows // 2, half), lambda b, t: (b, t, 0)),
        compiler_params=pltpu.CompilerParams(
            dimension_semantics=("arbitrary", "arbitrary"), vmem_limit_bytes=24 << 20
        ),
        cost_estimate=pl.CostEstimate(
            flops=0, bytes_accessed=4 * blocks * rows * half, transcendentals=0
        ),
        name="cp",
    )(matrix)


def solve_blocks(source, inverse):
    count = source.shape[0]
    pieces = source.reshape(count, inverse.shape[0], inverse.shape[1])
    result = jnp.einsum("bij,rbj->rbi", inverse, pieces, precision=lax.Precision.HIGHEST)
    return result.reshape(count, source.shape[1]).astype(jnp.bfloat16)


def line_slots(x, row, rows):
    left = right = x
    yield x, row, row >= 0, list(range(rows))

    def send(value, pairs):
        return lax.ppermute(value, "row", pairs)

    for step in range(1, rows):
        up = list(range(step - 1, rows - 1))
        down = list(range(1, rows - step + 1))
        from_left = [i + 1 for i in up]
        from_right = [i - 1 for i in down]
        up_pairs = [(i, i + 1) for i in up]
        down_pairs = [(i, i - 1) for i in down]
        if set(up) & set(down):
            left = send(left, up_pairs)
            right = send(right, down_pairs)
            if set(from_left) & set(from_right):
                yield left, jnp.maximum(row - step, 0), row >= step, from_left
                yield right, jnp.minimum(row + step, rows - 1), row + step < rows, from_right
                continue
            left = right = jnp.where(row >= step, left, right)
        else:
            left = right = send(left, up_pairs + down_pairs)
        block = jnp.where(row >= step, row - step, jnp.minimum(row + step, rows - 1))
        yield left, block, (row >= step) | (row + step < rows), from_left + from_right


def per_device(lag_matrix, past_current, excitation, block_inverse):
    lags, rows = lax.axis_size("lag"), lax.axis_size("row")
    lag, row = lax.axis_index("lag"), lax.axis_index("row")
    chips, chip, core = lags // 2, lag // 2, lag % 2
    matrix = lag_matrix[0]
    own = past_current[0]
    excite, width = own.shape
    half = width // 2
    blocks = block_inverse.shape[0] // 2
    share = excite // chips
    inverse = lax.dynamic_slice_in_dim(block_inverse, core * blocks, blocks, 0)
    drive = lax.dynamic_slice(
        excitation, (0, chip * share, core * half), (excitation.shape[0], share, half)
    )
    mate = [(i, i ^ 1) for i in range(lags)]

    def index(block, flag):
        return jnp.stack([block, core, flag.astype(jnp.int32), row * 0])

    def older(value, senders):
        pairs = [
            (k * rows + i, (k + 1) * rows + i) for k in range(lags - 1) for i in senders
        ]
        return lax.ppermute(value, ("lag", "row"), pairs)

    def halves(xs, idx, total, mates=None):
        (other,) = product(idx, xs, matrix, total, 0, mates=mates)
        got = lax.ppermute(other, "lag", mate)
        (mine,) = product(idx, xs, matrix, total, 1, mates=mates)
        return mine.reshape(chips, share, half), got.reshape(chips, share, half)

    def reduce_chips(mine, got):
        pick = lambda k: lax.dynamic_index_in_dim(
            mine, k, 0, keepdims=False
        ) + lax.dynamic_index_in_dim(got, k, 0, keepdims=False)
        total = pick(chip)
        for d in range(1, chips):
            total += lax.ppermute(pick(chip ^ d), "lag", [(i, i ^ (2 * d)) for i in range(lags)])
        return total

    seconds = second_halves(matrix, rows)
    mates = lax.ppermute(seconds, "lag", mate)

    total = None
    slots = list(line_slots(own, row, rows))
    for value, block, valid, senders in slots[:-1]:
        total = product(
            index(block, valid), [value, older(value, senders)], matrix, total, groups=2
        )
    value, block, valid, senders = slots[-1]
    late = index(block, valid)
    news = solve_blocks(drive[0] - reduce_chips(*halves([value], late, total[:1])), inverse)
    last = older(value, senders)

    far = [k for k in range(1, chips) if k & (k - 1)]
    near = [k for k in range(1, chips) if not k & (k - 1)]

    def to_first(x, k):
        return lax.ppermute(x, "lag", [(2 * k, 0), (2 * k + 1, 1)])

    def along(x, d, which):
        pairs = [
            ((2 * k + c) * rows + i, (2 * k + c) * rows + (i ^ d))
            for k in which
            for c in range(2)
            for i in range(rows)
        ]
        return lax.ppermute(x, ("lag", "row"), pairs)

    near_here = [to_first(news, k) for k in near]
    far_here = jnp.concatenate([to_first(news, k) for k in far], axis=0)
    away = [along(news, d, [0] + near) for d in range(1, rows)]
    far_away = [far_here] + [along(far_here, d, [0]) for d in range(1, rows)]
    stack = jnp.stack(away)
    near_away = [to_first(stack, k) for k in near]
    which = jnp.where(chip == 0, 1 + core, 0)
    order = [0] + far + near
    second = total[1:]
    for d in range(rows):
        one, close = (news, near_here) if d == 0 else (away[d - 1], [(x, d - 1) for x in near_away])
        fars = [far_away[d][j * share : (j + 1) * share] for j in range(len(far))]
        parts = [one] + fars + close
        parts = [parts[order.index(k)] for k in range(chips)]
        block = row ^ d
        idx = jnp.stack([2 * block, core, which, block])
        if d < rows - 1:
            second = product(idx, parts, matrix, second, mates=mates)
        else:
            pair = halves(parts, idx, second, mates)
        if d == 0:
            second = product(late, [last], matrix, second)
    finals = solve_blocks(drive[1] - reduce_chips(*pair), inverse)

    def assemble(x):
        count = share // 2
        keep = lax.dynamic_slice_in_dim(x, core * count, count, 0)
        give = lax.dynamic_slice_in_dim(x, (1 - core) * count, count, 0)
        got = lax.ppermute(give, "lag", mate)
        return jnp.concatenate(
            [jnp.where(core == 0, keep, got), jnp.where(core == 0, got, keep)], axis=1
        )

    return jnp.stack([assemble(news), assemble(finals)])


def solution(mesh):
    in_specs = (
        P("lag", "row", None),
        P("lag", None, "row"),
        P(None, None, "row"),
        P("row", None, None),
    )
    out_specs = P(None, "lag", "row")

    return jax.shard_map(
        per_device, mesh=mesh, in_specs=in_specs, out_specs=out_specs, check_vma=False
    )
```

time: 215 us -> 240 us (1.12)
  waiting for transfers between devices: 58.2 us -> 81.2 us
  Pallas kernels: 67.4 us -> 78.9 us
  starting transfers between devices: 67.3 us -> 58 us
  local copies, waits for them, and re-layouts: 12.2 us -> 7.68 us
  other arithmetic: 3.24 us -> 7.55 us
    ppermute x27 -> x19, waiting for transfers between devices: 55.9 us -> 80.2 us  [the longest x5 47.2 us: send(): return lax.ppermute(value, 'row', pairs)]
    ppermute x27 -> x19, starting transfers between devices: 39.8 us -> 25.5 us  [the longest x5 11 us: send(): return lax.ppermute(value, 'row', pairs)]
    pallas_call x0 -> x1, Pallas kernels: none -> 13.9 us  [second_halves(): pl.pallas_call(copy_kernel, out_shape=jax.ShapeDtypeStruct((blocks, rows,...]
    ppermute x6, starting transfers between devices: 15.9 us -> 20.6 us  [along(): return lax.ppermute(x, ('lag', 'row'), pairs)]
    slice x1 -> x0, local copies, waits for them, and re-layouts: 2.44 us -> none  [line_slots(): left = right = [x[k * cut:(k + 1) * cut] for k in range(PIECES)]]
    pallas_call x12, Pallas kernels: 67.4 us -> 65 us  [product(): pl.pallas_call(functools.partial(product_kernel, count=count, groups=grou...]
    ppermute x6 -> x5, starting transfers between devices: 9.32 us -> 10.8 us  [older(): return lax.ppermute(value, ('lag', 'row'), pairs)]
    unnamed x30 -> x36, local copies, waits for them, and re-layouts: 5.87 us -> 5.51 us
  transfers between devices with their start and end apart: 41 -> 32, of which waited for: 12 -> 11; matrix products, arithmetic and copies ran while one was open for 2% -> 5% of each run, Pallas kernels for 27% -> 25%
where the time goes in v1:
time: 240 us; the launch traced here: 239 us
  waiting for transfers between devices  81.2 us (34%)
  Pallas kernels  78.9 us (33%)
  starting transfers between devices  58 us (24%)
  local copies, waits for them, and re-layouts  7.68 us (3%)
  other arithmetic  7.55 us (3%)
  matrix products  4.63 us (2%)
    pallas_call x12, Pallas kernels, product(): pl.pallas_call(functools.partial(product_kernel, count=count, groups=grou...  65 us
    ppermute x5, waiting for transfers between devices, send(): return lax.ppermute(value, 'row', pairs)  47.2 us
    ppermute x6, waiting for transfers between devices, reduce_chips(): lax.ppermute(pick(chip ^ d), 'lag', [(i, i ^ 2 * d) for i in range(lags)])  28.7 us
    ppermute x6, starting transfers between devices, along(): return lax.ppermute(x, ('lag', 'row'), pairs)  20.6 us
    pallas_call x1, Pallas kernels, second_halves(): pl.pallas_call(copy_kernel, out_shape=jax.ShapeDtypeStruct((blocks, rows,...  13.9 us
    ppermute x5, starting transfers between devices, send(): return lax.ppermute(value, 'row', pairs)  11 us
    ppermute x5, starting transfers between devices, older(): return lax.ppermute(value, ('lag', 'row'), pairs)  10.8 us
    ppermute x6, starting transfers between devices, reduce_chips(): lax.ppermute(pick(chip ^ d), 'lag', [(i, i ^ 2 * d) for i in range(lags)])  7.09 us
  transfers between devices with their start and end apart: 32, of which 11 were waited for; matrix products, arithmetic and copies ran while one was open for 5% of the time, Pallas kernels for 25%

profile of v1, /device:TPU:0, one launch (start us, length us, event | category | flops | bytes accessed | tf_op | source)
XLA Modules:
  0.0 238.7 jit_solution(16091658182136256158)
XLA Ops:
  0.0 13.9 %cp.1 = bf16[4,2048,1024]{2,1,0:T(8,128)(2,1)} custom-call(bf16[2048,8192]{1,0:T(8,128)(2,1)} %bitcast.117), custom_call_target="tpu_custom_call" | custom-call | bytes 33554432 | tf_op jit(solution)/shard_map/cp/pallas_call | solution.py:132
  14.4 5.4 %collective-permute-start = (bf16[256,2048]{1,0:T(8,128)(2,1)S(1)}, bf16[256,2048]{1,0:T(8,128)(2,1)}, u32[]{:S(2)}, u32[]{:S(2)}) collective-permute-start(bf16[256,2048]{1,0:T(8,128)(2,1)S(1)} %bitcast.111), channel_id=1, source_target_pairs={{0,1},{1,2},{2,3},{4,5},{5,6},{6,7},{8,9},{9,10},{10,11},{12,13},{... | collective-permute-start | bytes 3145736 | tf_op jit(solution)/shard_map/ppermute | solution.py:160
  21.1 20.8 %collective-permute-done.refs_0_ = bf16[256,2048]{1,0:T(8,128)(2,1)} collective-permute-done((bf16[256,2048]{1,0:T(8,128)(2,1)S(1)}, bf16[256,2048]{1,0:T(8,128)(2,1)}, u32[]{:S(2)}, u32[]{:S(2)}) %collective-permute-start) | collective-permute-done | bytes 1048608 | tf_op jit(solution)/shard_map/ppermute | solution.py:160
  43.6 3.5 %collective-permute-done.2.refs_0_ = bf16[256,2048]{1,0:T(8,128)(2,1)} collective-permute-done((bf16[256,2048]{1,0:T(8,128)(2,1)S(1)}, bf16[256,2048]{1,0:T(8,128)(2,1)}, u32[]{:S(2)}, u32[]{:S(2)}) %collective-permute-start.2) | collective-permute-done | bytes 1048608 | tf_op jit(solution)/shard_map/ppermute | solution.py:160
  51.8 4.1 %collective-permute-start.6 = (bf16[256,2048]{1,0:T(8,128)(2,1)}, bf16[256,2048]{1,0:T(8,128)(2,1)S(1)}, u32[]{:S(2)}, u32[]{:S(2)}) collective-permute-start(bf16[256,2048]{1,0:T(8,128)(2,1)} %collective-permute-done.2.refs_0_), channel_id=1, source_target_pairs={{0,4},{1,5},{2,6},{4,8},{5,9},{6,10},{8,12},{9,13},{10,14},{12,16}... | collective-permute-start | bytes 3145736 | tf_op jit(solution)/shard_map/ppermute | solution.py:206
  56.0 18.0 %collective-permute-done.3 = bf16[256,2048]{1,0:T(8,128)(2,1)} collective-permute-done((bf16[256,2048]{1,0:T(8,128)(2,1)}, bf16[256,2048]{1,0:T(8,128)(2,1)}, u32[]{:S(2)}, u32[]{:S(2)}) %collective-permute-start.3) | collective-permute-done | bytes 1048608 | tf_op jit(solution)/shard_map/ppermute | solution.py:160
  76.7 7.6 %shard_map.46 = (f32[2,256,1024]{2,1,0:T(8,128)S(1)}, f32[2,256,1024]{2,1,0:T(8,128)S(1)}) custom-call(s32[4]{0:T(128)S(1)} %pad_add_fusion.idx, bf16[256,2048]{1,0:T(8,128)(2,1)S(1)} %bitcast.114, bf16[256,2048]{1,0:T(8,128)(2,1)S(1)} %collective-permute-done.8.refs_1_, bf16[2048,8192]{1,0:T(8,128)(2,1)} %bitcast.118), custom_call_target="tpu_custom_call" | custom-call | flops 4294967296 | bytes 16777216 | tf_op jit(solution)/shard_map/pallas_call | solution.py:99
  85.6 4.8 %shard_map.47 = (f32[2,256,1024]{2,1,0:T(8,128)S(1)}, f32[2,256,1024]{2,1,0:T(8,128)S(1)}) custom-call(s32[4]{0:T(128)S(1)} %pad_add_fusion.1.idx, bf16[256,2048]{1,0:T(8,128)(2,1)} %collective-permute-done.refs_0_, bf16[256,2048]{1,0:T(8,128)(2,1)} %collective-permute-done.7.refs_1_, bf16[2048,8192]{1,0:T(8,128)(2,1)} %bitcast.119, ...), custom_call_target="tpu_custom_call" | custom-call | flops 4294967296 | bytes 16777216 | tf_op jit(solution)/shard_map/pallas_call | solution.py:99
  90.5 8.0 %shard_map.48 = (f32[2,256,1024]{2,1,0:T(8,128)S(1)}, f32[2,256,1024]{2,1,0:T(8,128)S(1)}) custom-call(s32[4]{0:T(128)S(1)} %pad_add_fusion.2.idx, bf16[256,2048]{1,0:T(8,128)(2,1)} %collective-permute-done.2.refs_0_, bf16[256,2048]{1,0:T(8,128)(2,1)S(1)} %collective-permute-done.6.refs_1_, bf16[2048,8192]{1,0:T(8,128)(2,1)} %bitcast.120, ...), custom_call_target="tpu_custom_call" | custom-call | flops 4294967296 | bytes 16777216 | tf_op jit(solution)/shard_map/pallas_call | solution.py:99
  98.5 7.7 %shard_map.49 = (f32[2,256,1024]{2,1,0:T(8,128)S(1)}, f32[2,256,1024]{2,1,0:T(8,128)S(1)}) custom-call(s32[4]{0:T(128)S(1)} %pad_add_fusion.3.idx, bf16[256,2048]{1,0:T(8,128)(2,1)S(1)} %broadcast_select_fusion.refs_0_, bf16[256,2048]{1,0:T(8,128)(2,1)S(1)} %collective-permute-done.5.refs_1_, bf16[2048,8192]{1,0:T(8,128)(2,1)} %bitcast.121, ...), custom_call_target="tpu_custom_call" | custom-call | flops 4294967296 | bytes 16777216 | tf_op jit(solution)/shard_map/pallas_call | solution.py:99
  106.2 5.0 %collective-permute-done.4.refs_0_ = bf16[256,2048]{1,0:T(8,128)(2,1)} collective-permute-done((bf16[256,2048]{1,0:T(8,128)(2,1)S(1)}, bf16[256,2048]{1,0:T(8,128)(2,1)}, u32[]{:S(2)}, u32[]{:S(2)}) %collective-permute-start.4) | collective-permute-done | bytes 1048608 | tf_op jit(solution)/shard_map/ppermute | solution.py:160
  111.1 5.3 %shard_map.51 = f32[1,256,1024]{2,1,0:T(8,128)} custom-call(s32[4]{0:T(128)S(1)} %pad_add_fusion.4.idx, bf16[256,2048]{1,0:T(8,128)(2,1)} %collective-permute-done.4.refs_0_, bf16[2048,8192]{1,0:T(8,128)(2,1)} %bitcast.122, f32[2,256,1024]{2,1,0:T(8,128)S(1)} %get-tuple-element.19.refs_2_), custom_call_target="tpu_custom_call" | custom-call | flops 1073741824 | bytes 6291456 | tf_op jit(solution)/shard_map/pallas_call | solution.py:99
  117.5 4.3 %shard_map.50 = f32[1,256,1024]{2,1,0:T(8,128)S(1)} custom-call(s32[4]{0:T(128)S(1)} %pad_add_fusion.4.idx, bf16[256,2048]{1,0:T(8,128)(2,1)} %collective-permute-done.4.refs_0_, bf16[2048,8192]{1,0:T(8,128)(2,1)} %bitcast.123, f32[2,256,1024]{2,1,0:T(8,128)S(1)} %get-tuple-element.19.refs_2_), custom_call_target="tpu_custom_call" | custom-call | flops 1073741824 | bytes 6291456 | tf_op jit(solution)/shard_map/pallas_call | solution.py:99
  124.9 2.1 collective-permute-start.10
  128.4 2.4 collective-permute-start.24
  130.8 3.5 %collective-permute-done.10 = f32[64,1024]{1,0:T(8,128)S(1)} collective-permute-done((f32[64,1024]{1,0:T(8,128)}, f32[64,1024]{1,0:T(8,128)S(1)}, u32[]{:S(2)}, u32[]{:S(2)}) %collective-permute-start.10) | collective-permute-done | bytes 262176 | tf_op jit(solution)/shard_map/ppermute | solution.py:220
  134.3 15.7 %collective-permute-done.11 = f32[64,1024]{1,0:T(8,128)} collective-permute-done((f32[64,1024]{1,0:T(8,128)}, f32[64,1024]{1,0:T(8,128)}, u32[]{:S(2)}, u32[]{:S(2)}) %collective-permute-start.11) | collective-permute-done | bytes 262176 | tf_op jit(solution)/shard_map/ppermute | solution.py:220
  150.0 2.4 %fusion = bf16[8,8,8,128]{3,2,1,0:T(8,128)(2,1)S(1)} fusion(f32[16,128,128]{2,1,0:T(8,128)S(1)} %copy-done, s32[]{:T(128)S(6)} %select_n.104, f32[2,256,2048]{2,1,0:T(8,128)} %param.6, s32[]{:T(128)S(6)} %select_n.94, s32[]{:T(128)S(6)} %select_n.95, f32[64,1024]{1,0:T(8,128)} %collective-permute-done.12, f32[64,1024]{1,0:T(8,128)} %collective-permute-done.11, ...), kind=kOutput, calls=%fused_computation.2 | convolution fusion | flops 101056512 | bytes 2228240 | tf_op jit(solution)/shard_map/bij,rbj->rbi/dot_general | solution.py:151
  157.6 6.3 %collective-permute-start.14 = (bf16[64,1024]{1,0:T(8,128)(2,1)}, bf16[64,1024]{1,0:T(8,128)(2,1)S(1)}, u32[]{:S(2)}, u32[]{:S(2)}) collective-permute-start(bf16[64,1024]{1,0:T(8,128)(2,1)} %bitcast.105.refs_0_), channel_id=1, source_target_pairs={{0,3},{1,2},{2,1},{3,0},{4,7},{5,6},{6,5},{7,4},{8,11},{9,10},{10,... | collective-permute-start | bytes 393224 | tf_op jit(solution)/shard_map/ppermute | solution.py:250
  168.9 3.0 %collective-permute-done.19.refs_3_ = bf16[64,1024]{1,0:T(8,128)(2,1)} collective-permute-done((bf16[64,1024]{1,0:T(8,128)(2,1)}, bf16[64,1024]{1,0:T(8,128)(2,1)}, u32[]{:S(2)}, u32[]{:S(2)}) %collective-permute-start.19) | collective-permute-done | bytes 131104 | tf_op jit(solution)/shard_map/ppermute | solution.py:241
  174.7 2.3 collective-permute-start.23
  177.0 6.2 %collective-permute-start.22 = (bf16[64,1024]{1,0:T(8,128)(2,1)}, bf16[64,1024]{1,0:T(8,128)(2,1)S(1)}, u32[]{:S(2)}, u32[]{:S(2)}) collective-permute-start(bf16[64,1024]{1,0:T(8,128)(2,1)} %collective-permute-done.19.refs_3_), channel_id=1, source_target_pairs={{0,2},{1,3},{2,0},{3,1},{4,6},{5,7},{6,4},{7,5}} | collective-permute-start | bytes 393224 | tf_op jit(solution)/shard_map/ppermute | solution.py:250
  183.9 4.5 %shard_map.52.refs_2_ = f32[2,256,1024]{2,1,0:T(8,128)S(1)} custom-call(s32[4]{0:T(128)S(1)} %copy-done.17, bf16[64,1024]{1,0:T(8,128)(2,1)} %bitcast.105.refs_0_, bf16[64,1024]{1,0:T(8,128)(2,1)} %collective-permute-done.25.refs_1_, bf16[64,1024]{1,0:T(8,128)(2,1)S(1)} %collective-permute-done.26.refs_2_, bf16[64,1024]{1,0:T(8,128)(2,1)} %collective-permute-done.19.refs_3_, ...), custom_call_target="tpu_custom_call" | custom-call | flops 1073741824 | bytes 8388608 | tf_op jit(solution)/shard_map/pallas_call | solution.py:99
  190.5 5.7 %shard_map.53.refs_6_ = f32[2,256,1024]{2,1,0:T(8,128)S(1)} custom-call(s32[4]{0:T(128)S(1)} %pad_add_fusion.4.idx, bf16[256,2048]{1,0:T(8,128)(2,1)} %collective-permute-done.24.refs_0_, bf16[2048,8192]{1,0:T(8,128)(2,1)} %bitcast.125, f32[2,256,1024]{2,1,0:T(8,128)S(1)} %shard_map.52.refs_2_), custom_call_target="tpu_custom_call" | custom-call | flops 2147483648 | bytes 12582912 | tf_op jit(solution)/shard_map/pallas_call | solution.py:99
  196.2 4.4 %shard_map.54.refs_6_ = f32[2,256,1024]{2,1,0:T(8,128)S(1)} custom-call(s32[4]{0:T(128)S(1)} %pad_add_fusion.7.idx, bf16[64,1024]{1,0:T(8,128)(2,1)S(1)} %copy-done.16, bf16[3,64,1024]{2,1,0:T(8,128)(2,1)S(1)} %collective-permute-done.17.refs_1_, bf16[3,64,1024]{2,1,0:T(8,128)(2,1)S(1)} %collective-permute-done.18.refs_2_, ...), custom_call_target="tpu_custom_call" | custom-call | flops 1073741824 | bytes 8388608 | tf_op jit(solution)/shard_map/pallas_call | solution.py:99
  200.7 4.4 %shard_map.55.refs_6_ = f32[2,256,1024]{2,1,0:T(8,128)S(1)} custom-call(s32[4]{0:T(128)S(1)} %pad_add_fusion.6.idx, bf16[64,1024]{1,0:T(8,128)(2,1)S(1)} %copy-done.14, bf16[3,64,1024]{2,1,0:T(8,128)(2,1)S(1)} %collective-permute-done.17.refs_1_, bf16[3,64,1024]{2,1,0:T(8,128)(2,1)S(1)} %collective-permute-done.18.refs_2_, ...), custom_call_target="tpu_custom_call" | custom-call | flops 1073741824 | bytes 8388608 | tf_op jit(solution)/shard_map/pallas_call | solution.py:99
  205.2 4.5 %shard_map.57 = f32[1,256,1024]{2,1,0:T(8,128)} custom-call(s32[4]{0:T(128)S(1)} %pad_add_fusion.5.idx, bf16[64,1024]{1,0:T(8,128)(2,1)S(1)} %copy-done.8, bf16[3,64,1024]{2,1,0:T(8,128)(2,1)S(1)} %collective-permute-done.17.refs_1_, bf16[3,64,1024]{2,1,0:T(8,128)(2,1)S(1)} %collective-permute-done.18.refs_2_, ...), custom_call_target="tpu_custom_call" | custom-call | flops 536870912 | bytes 4194304 | tf_op jit(solution)/shard_map/pallas_call | solution.py:99
  214.5 3.6 %shard_map.56 = f32[1,256,1024]{2,1,0:T(8,128)S(1)} custom-call(s32[4]{0:T(128)S(1)} %pad_add_fusion.5.idx, bf16[64,1024]{1,0:T(8,128)(2,1)S(1)} %copy-done.9, bf16[3,64,1024]{2,1,0:T(8,128)(2,1)S(1)} %collective-permute-done.17.refs_1_, bf16[3,64,1024]{2,1,0:T(8,128)(2,1)S(1)} %copy-done.2, bf16[64,1024]{1,0:T(8,128)(2,1)S(1)} %copy-done.12, ...), custom_call_target="tpu_custom_call" | custom-call | flops 536870912 | bytes 4194304 | tf_op jit(solution)/shard_map/pallas_call | solution.py:99
  220.5 3.4 %collective-permute-start.30 = (f32[64,1024]{1,0:T(8,128)S(1)}, f32[64,1024]{1,0:T(8,128)S(1)}, u32[]{:S(2)}, u32[]{:S(2)}) collective-permute-start(f32[64,1024]{1,0:T(8,128)S(1)} %get-tuple-element.22), channel_id=1, source_target_pairs={{0,24},{4,28},{8,16},{12,20},{16,8},{20,12},{24,0},{28,4},{1,25},{... | collective-permute-start | bytes 786440 | tf_op jit(solution)/shard_map/ppermute | solution.py:220
  224.8 4.8 %collective-permute-done.28 = f32[64,1024]{1,0:T(8,128)S(1)} collective-permute-done((f32[64,1024]{1,0:T(8,128)S(1)}, f32[64,1024]{1,0:T(8,128)S(1)}, u32[]{:S(2)}, u32[]{:S(2)}) %collective-permute-start.28) | collective-permute-done | bytes 262176 | tf_op jit(solution)/shard_map/ppermute | solution.py:220
  229.6 4.7 %collective-permute-done.29 = f32[64,1024]{1,0:T(8,128)S(1)} collective-permute-done((f32[64,1024]{1,0:T(8,128)S(1)}, f32[64,1024]{1,0:T(8,128)S(1)}, u32[]{:S(2)}, u32[]{:S(2)}) %collective-permute-start.29) | collective-permute-done | bytes 262176 | tf_op jit(solution)/shard_map/ppermute | solution.py:220
  234.3 2.2 fusion.1
  (105 shorter events, 43.4 us)
Async XLA Ops:
  13.9 163.1 %collective-permute-start.21 = (bf16[4,2048,1024]{2,1,0:T(8,128)(2,1)}, bf16[4,2048,1024]{2,1,0:T(8,128)(2,1)}, u32[]{:S(2)}, u32[]{:S(2)}) collective-permute-start(bf16[4,2048,1024]{2,1,0:T(8,128)(2,1)} %cp.1), channel_id=1, source_target_pairs={{0,4},{4,0},{8,12},{12,8},{16,20},{20,16},{24,28},{28,24},{1,5},{5... | collective-permute-start | bytes 50331656 | tf_op jit(solution)/shard_map/ppermute | solution.py:224
  14.4 27.5 %collective-permute-start = (bf16[256,2048]{1,0:T(8,128)(2,1)S(1)}, bf16[256,2048]{1,0:T(8,128)(2,1)}, u32[]{:S(2)}, u32[]{:S(2)}) collective-permute-start(bf16[256,2048]{1,0:T(8,128)(2,1)S(1)} %bitcast.111), channel_id=1, source_target_pairs={{0,1},{1,2},{2,3},{4,5},{5,6},{6,7},{8,9},{9,10},{10,11},{12,13},{... | collective-permute-start | bytes 3145736 | tf_op jit(solution)/shard_map/ppermute | solution.py:160
  19.9 27.3 %collective-permute-start.2 = (bf16[256,2048]{1,0:T(8,128)(2,1)S(1)}, bf16[256,2048]{1,0:T(8,128)(2,1)}, u32[]{:S(2)}, u32[]{:S(2)}) collective-permute-start(bf16[256,2048]{1,0:T(8,128)(2,1)S(1)} %bitcast.112), channel_id=1, source_target_pairs={{1,0},{2,1},{3,2},{5,4},{6,5},{7,6},{9,8},{10,9},{11,10},{13,12},{... | collective-permute-start | bytes 3145736 | tf_op jit(solution)/shard_map/ppermute | solution.py:160
  42.0 9.9 %collective-permute-start.1 = (bf16[256,2048]{1,0:T(8,128)(2,1)}, bf16[256,2048]{1,0:T(8,128)(2,1)}, u32[]{:S(2)}, u32[]{:S(2)}) collective-permute-start(bf16[256,2048]{1,0:T(8,128)(2,1)} %collective-permute-done.refs_0_), channel_id=1, source_target_pairs={{1,2},{2,3},{5,6},{6,7},{9,10},{10,11},{13,14},{14,15},{17,18},{18... | collective-permute-start | bytes 3145736 | tf_op jit(solution)/shard_map/ppermute | solution.py:160
  47.1 26.8 %collective-permute-start.3 = (bf16[256,2048]{1,0:T(8,128)(2,1)}, bf16[256,2048]{1,0:T(8,128)(2,1)}, u32[]{:S(2)}, u32[]{:S(2)}) collective-permute-start(bf16[256,2048]{1,0:T(8,128)(2,1)} %collective-permute-done.2.refs_0_), channel_id=1, source_target_pairs={{1,0},{2,1},{5,4},{6,5},{9,8},{10,9},{13,12},{14,13},{17,16},{18,1... | collective-permute-start | bytes 3145736 | tf_op jit(solution)/shard_map/ppermute | solution.py:160
  48.4 28.2 %collective-permute-start.8 = (bf16[256,2048]{1,0:T(8,128)(2,1)S(1)}, bf16[256,2048]{1,0:T(8,128)(2,1)S(1)}, u32[]{:S(2)}, u32[]{:S(2)}) collective-permute-start(bf16[256,2048]{1,0:T(8,128)(2,1)S(1)} %bitcast.113), channel_id=1, source_target_pairs={{0,4},{1,5},{2,6},{3,7},{4,8},{5,9},{6,10},{7,11},{8,12},{9,13},{1... | collective-permute-start | bytes 3145736 | tf_op jit(solution)/shard_map/ppermute | solution.py:206
  50.1 35.6 %collective-permute-start.7 = (bf16[256,2048]{1,0:T(8,128)(2,1)}, bf16[256,2048]{1,0:T(8,128)(2,1)}, u32[]{:S(2)}, u32[]{:S(2)}) collective-permute-start(bf16[256,2048]{1,0:T(8,128)(2,1)} %collective-permute-done.refs_0_), channel_id=1, source_target_pairs={{1,5},{2,6},{3,7},{5,9},{6,10},{7,11},{9,13},{10,14},{11,15},{13,1... | collective-permute-start | bytes 3145736 | tf_op jit(solution)/shard_map/ppermute | solution.py:206
  51.8 38.6 %collective-permute-start.6 = (bf16[256,2048]{1,0:T(8,128)(2,1)}, bf16[256,2048]{1,0:T(8,128)(2,1)S(1)}, u32[]{:S(2)}, u32[]{:S(2)}) collective-permute-start(bf16[256,2048]{1,0:T(8,128)(2,1)} %collective-permute-done.2.refs_0_), channel_id=1, source_target_pairs={{0,4},{1,5},{2,6},{4,8},{5,9},{6,10},{8,12},{9,13},{10,14},{12,16}... | collective-permute-start | bytes 3145736 | tf_op jit(solution)/shard_map/ppermute | solution.py:206
  75.3 23.2 %collective-permute-start.5 = (bf16[256,2048]{1,0:T(8,128)(2,1)S(1)}, bf16[256,2048]{1,0:T(8,128)(2,1)S(1)}, u32[]{:S(2)}, u32[]{:S(2)}) collective-permute-start(bf16[256,2048]{1,0:T(8,128)(2,1)S(1)} %broadcast_select_fusion.refs_0_), channel_id=1, source_target_pairs={{2,6},{3,7},{0,4},{1,5},{6,10},{7,11},{4,8},{5,9},{10,14},{11,15},... | collective-permute-start | bytes 3145736 | tf_op jit(solution)/shard_map/ppermute | solution.py:206
  84.3 26.8 %collective-permute-start.4 = (bf16[256,2048]{1,0:T(8,128)(2,1)S(1)}, bf16[256,2048]{1,0:T(8,128)(2,1)}, u32[]{:S(2)}, u32[]{:S(2)}) collective-permute-start(bf16[256,2048]{1,0:T(8,128)(2,1)S(1)} %broadcast_select_fusion.refs_0_), channel_id=1, source_target_pairs={{2,3},{1,0},{6,7},{5,4},{10,11},{9,8},{14,15},{13,12},{18,19},{17,... | collective-permute-start | bytes 3145736 | tf_op jit(solution)/shard_map/ppermute | solution.py:160
  116.5 5.4 %collective-permute-start.9 = (f32[1,256,1024]{2,1,0:T(8,128)}, f32[1,256,1024]{2,1,0:T(8,128)}, u32[]{:S(2)}, u32[]{:S(2)}) collective-permute-start(f32[1,256,1024]{2,1,0:T(8,128)} %shard_map.51), channel_id=1, source_target_pairs={{0,4},{4,0},{8,12},{12,8},{16,20},{20,16},{24,28},{28,24},{1,5},{5... | collective-permute-start | bytes 3145736 | tf_op jit(solution)/shard_map/ppermute | solution.py:210
  124.9 9.4 %collective-permute-start.10 = (f32[64,1024]{1,0:T(8,128)}, f32[64,1024]{1,0:T(8,128)S(1)}, u32[]{:S(2)}, u32[]{:S(2)}) collective-permute-start(f32[64,1024]{1,0:T(8,128)} %get-tuple-element.24), channel_id=1, source_target_pairs={{0,8},{4,12},{8,0},{12,4},{16,24},{20,28},{24,16},{28,20},{1,9},{5... | collective-permute-start | bytes 786440 | tf_op jit(solution)/shard_map/ppermute | solution.py:220
  126.9 23.0 %collective-permute-start.11 = (f32[64,1024]{1,0:T(8,128)}, f32[64,1024]{1,0:T(8,128)}, u32[]{:S(2)}, u32[]{:S(2)}) collective-permute-start(f32[64,1024]{1,0:T(8,128)} %get-tuple-element.26), channel_id=1, source_target_pairs={{0,16},{4,20},{8,24},{12,28},{16,0},{20,4},{24,8},{28,12},{1,17},{... | collective-permute-start | bytes 786440 | tf_op jit(solution)/shard_map/ppermute | solution.py:220
  127.0 23.0 %collective-permute-start.12 = (f32[64,1024]{1,0:T(8,128)}, f32[64,1024]{1,0:T(8,128)}, u32[]{:S(2)}, u32[]{:S(2)}) collective-permute-start(f32[64,1024]{1,0:T(8,128)} %get-tuple-element.25), channel_id=1, source_target_pairs={{0,24},{4,28},{8,16},{12,20},{16,8},{20,12},{24,0},{28,4},{1,25},{... | collective-permute-start | bytes 786440 | tf_op jit(solution)/shard_map/ppermute | solution.py:220
  128.4 60.0 %collective-permute-start.24 = (bf16[256,2048]{1,0:T(8,128)(2,1)}, bf16[256,2048]{1,0:T(8,128)(2,1)}, u32[]{:S(2)}, u32[]{:S(2)}) collective-permute-start(bf16[256,2048]{1,0:T(8,128)(2,1)} %collective-permute-done.4.refs_0_), channel_id=1, source_target_pairs={{3,7},{0,4},{7,11},{4,8},{11,15},{8,12},{15,19},{12,16},{19,23},{1... | collective-permute-start | bytes 3145736 | tf_op jit(solution)/shard_map/ppermute | solution.py:206
  153.1 10.9 %collective-permute-start.15 = (bf16[64,1024]{1,0:T(8,128)(2,1)}, bf16[64,1024]{1,0:T(8,128)(2,1)S(1)}, u32[]{:S(2)}, u32[]{:S(2)}) collective-permute-start(bf16[64,1024]{1,0:T(8,128)(2,1)} %bitcast.105.refs_0_), channel_id=1, source_target_pairs={{0,1},{1,0},{2,3},{3,2},{4,5},{5,4},{6,7},{7,6},{8,9},{9,8},{10,11... | collective-permute-start | bytes 393224 | tf_op jit(solution)/shard_map/ppermute | solution.py:250
  155.0 10.2 %collective-permute-start.16 = (bf16[64,1024]{1,0:T(8,128)(2,1)}, bf16[64,1024]{1,0:T(8,128)(2,1)S(1)}, u32[]{:S(2)}, u32[]{:S(2)}) collective-permute-start(bf16[64,1024]{1,0:T(8,128)(2,1)} %bitcast.105.refs_0_), channel_id=1, source_target_pairs={{0,2},{1,3},{2,0},{3,1},{4,6},{5,7},{6,4},{7,5},{8,10},{9,11},{10,... | collective-permute-start | bytes 393224 | tf_op jit(solution)/shard_map/ppermute | solution.py:250
  157.6 10.0 %collective-permute-start.14 = (bf16[64,1024]{1,0:T(8,128)(2,1)}, bf16[64,1024]{1,0:T(8,128)(2,1)S(1)}, u32[]{:S(2)}, u32[]{:S(2)}) collective-permute-start(bf16[64,1024]{1,0:T(8,128)(2,1)} %bitcast.105.refs_0_), channel_id=1, source_target_pairs={{0,3},{1,2},{2,1},{3,0},{4,7},{5,6},{6,5},{7,4},{8,11},{9,10},{10,... | collective-permute-start | bytes 393224 | tf_op jit(solution)/shard_map/ppermute | solution.py:250
  163.9 8.1 %collective-permute-start.19 = (bf16[64,1024]{1,0:T(8,128)(2,1)}, bf16[64,1024]{1,0:T(8,128)(2,1)}, u32[]{:S(2)}, u32[]{:S(2)}) collective-permute-start(bf16[64,1024]{1,0:T(8,128)(2,1)} %bitcast.105.refs_0_), channel_id=1, source_target_pairs={{24,0},{28,4},{25,1},{29,5},{26,2},{30,6},{27,3},{31,7}} | collective-permute-start | bytes 393224 | tf_op jit(solution)/shard_map/ppermute | solution.py:241
  165.2 8.0 %collective-permute-start.25 = (bf16[64,1024]{1,0:T(8,128)(2,1)}, bf16[64,1024]{1,0:T(8,128)(2,1)}, u32[]{:S(2)}, u32[]{:S(2)}) collective-permute-start(bf16[64,1024]{1,0:T(8,128)(2,1)} %bitcast.105.refs_0_), channel_id=1, source_target_pairs={{8,0},{12,4},{9,1},{13,5},{10,2},{14,6},{11,3},{15,7}} | collective-permute-start | bytes 393224 | tf_op jit(solution)/shard_map/ppermute | solution.py:241
  167.6 7.1 %collective-permute-start.26 = (bf16[64,1024]{1,0:T(8,128)(2,1)}, bf16[64,1024]{1,0:T(8,128)(2,1)S(1)}, u32[]{:S(2)}, u32[]{:S(2)}) collective-permute-start(bf16[64,1024]{1,0:T(8,128)(2,1)} %bitcast.105.refs_0_), channel_id=1, source_target_pairs={{16,0},{20,4},{17,1},{21,5},{18,2},{22,6},{19,3},{23,7}} | collective-permute-start | bytes 393224 | tf_op jit(solution)/shard_map/ppermute | solution.py:241
  172.0 24.2 %collective-permute-start.17 = (bf16[3,64,1024]{2,1,0:T(8,128)(2,1)S(1)}, bf16[3,64,1024]{2,1,0:T(8,128)(2,1)S(1)}, u32[]{:S(2)}, u32[]{:S(2)}) collective-permute-start(bf16[3,64,1024]{2,1,0:T(8,128)(2,1)S(1)} %pad_maximum_fusion), channel_id=1, source_target_pairs={{8,0},{12,4},{9,1},{13,5},{10,2},{14,6},{11,3},{15,7}} | collective-permute-start | bytes 1179656 | tf_op jit(solution)/shard_map/ppermute | solution.py:241
  173.3 22.9 %collective-permute-start.18 = (bf16[3,64,1024]{2,1,0:T(8,128)(2,1)S(1)}, bf16[3,64,1024]{2,1,0:T(8,128)(2,1)S(1)}, u32[]{:S(2)}, u32[]{:S(2)}) collective-permute-start(bf16[3,64,1024]{2,1,0:T(8,128)(2,1)S(1)} %pad_maximum_fusion), channel_id=1, source_target_pairs={{16,0},{20,4},{17,1},{21,5},{18,2},{22,6},{19,3},{23,7}} | collective-permute-start | bytes 1179656 | tf_op jit(solution)/shard_map/ppermute | solution.py:241
  174.7 21.5 %collective-permute-start.23 = (bf16[64,1024]{1,0:T(8,128)(2,1)}, bf16[64,1024]{1,0:T(8,128)(2,1)S(1)}, u32[]{:S(2)}, u32[]{:S(2)}) collective-permute-start(bf16[64,1024]{1,0:T(8,128)(2,1)} %collective-permute-done.19.refs_3_), channel_id=1, source_target_pairs={{0,1},{1,0},{2,3},{3,2},{4,5},{5,4},{6,7},{7,6}} | collective-permute-start | bytes 393224 | tf_op jit(solution)/shard_map/ppermute | solution.py:250
  177.0 23.7 %collective-permute-start.22 = (bf16[64,1024]{1,0:T(8,128)(2,1)}, bf16[64,1024]{1,0:T(8,128)(2,1)S(1)}, u32[]{:S(2)}, u32[]{:S(2)}) collective-permute-start(bf16[64,1024]{1,0:T(8,128)(2,1)} %collective-permute-done.19.refs_3_), channel_id=1, source_target_pairs={{0,2},{1,3},{2,0},{3,1},{4,6},{5,7},{6,4},{7,5}} | collective-permute-start | bytes 393224 | tf_op jit(solution)/shard_map/ppermute | solution.py:250
  188.4 16.7 %collective-permute-start.20 = (bf16[64,1024]{1,0:T(8,128)(2,1)}, bf16[64,1024]{1,0:T(8,128)(2,1)S(1)}, u32[]{:S(2)}, u32[]{:S(2)}) collective-permute-start(bf16[64,1024]{1,0:T(8,128)(2,1)} %collective-permute-done.19.refs_3_), channel_id=1, source_target_pairs={{0,3},{1,2},{2,1},{3,0},{4,7},{5,6},{6,5},{7,4}} | collective-permute-start | bytes 393224 | tf_op jit(solution)/shard_map/ppermute | solution.py:250
  209.7 8.4 %collective-permute-start.27 = (f32[1,256,1024]{2,1,0:T(8,128)}, f32[1,256,1024]{2,1,0:T(8,128)}, u32[]{:S(2)}, u32[]{:S(2)}) collective-permute-start(f32[1,256,1024]{2,1,0:T(8,128)} %shard_map.57), channel_id=1, source_target_pairs={{0,4},{4,0},{8,12},{12,8},{16,20},{20,16},{24,28},{28,24},{1,5},{5... | collective-permute-start | bytes 3145736 | tf_op jit(solution)/shard_map/ppermute | solution.py:210
  211.2 12.7 %collective-permute-start.13 = (bf16[32,1024]{1,0:T(8,128)(2,1)}, bf16[32,1024]{1,0:T(8,128)(2,1)}, u32[]{:S(2)}, u32[]{:S(2)}) collective-permute-start(bf16[32,1024]{1,0:T(8,128)(2,1)} %constant_dynamic-slice_fusion.1), channel_id=1, source_target_pairs={{0,4},{4,0},{8,12},{12,8},{16,20},{20,16},{24,28},{28,24},{1,5},{5... | collective-permute-start | bytes 196616 | tf_op jit(solution)/shard_map/ppermute | solution.py:280
  220.3 9.2 %collective-permute-start.28 = (f32[64,1024]{1,0:T(8,128)S(1)}, f32[64,1024]{1,0:T(8,128)S(1)}, u32[]{:S(2)}, u32[]{:S(2)}) collective-permute-start(f32[64,1024]{1,0:T(8,128)S(1)} %get-tuple-element.21), channel_id=1, source_target_pairs={{0,8},{4,12},{8,0},{12,4},{16,24},{20,28},{24,16},{28,20},{1,9},{5... | collective-permute-start | bytes 786440 | tf_op jit(solution)/shard_map/ppermute | solution.py:220
  220.4 13.9 %collective-permute-start.29 = (f32[64,1024]{1,0:T(8,128)S(1)}, f32[64,1024]{1,0:T(8,128)S(1)}, u32[]{:S(2)}, u32[]{:S(2)}) collective-permute-start(f32[64,1024]{1,0:T(8,128)S(1)} %get-tuple-element.23), channel_id=1, source_target_pairs={{0,16},{4,20},{8,24},{12,28},{16,0},{20,4},{24,8},{28,12},{1,17},{... | collective-permute-start | bytes 786440 | tf_op jit(solution)/shard_map/ppermute | solution.py:220
  220.5 13.8 %collective-permute-start.30 = (f32[64,1024]{1,0:T(8,128)S(1)}, f32[64,1024]{1,0:T(8,128)S(1)}, u32[]{:S(2)}, u32[]{:S(2)}) collective-permute-start(f32[64,1024]{1,0:T(8,128)S(1)} %get-tuple-element.22), channel_id=1, source_target_pairs={{0,24},{4,28},{8,16},{12,20},{16,8},{20,12},{24,0},{28,4},{1,25},{... | collective-permute-start | bytes 786440 | tf_op jit(solution)/shard_map/ppermute | solution.py:220
  236.6 1.3 collective-permute-start.31
  (18 other events, 279.0 us)
